TPU v7x, 128 devices: a whole 4x4x4 slice. The times are simulated.
128 devices in a mesh: row: 8 (over x_hi, z), col: 16 (over y, x_lo, core).
Axes of the slice: x: 4 (x_hi: 2, x_lo: 2; x = x_hi * 2 + x_lo), y: 4, z: 4, core: 2. Of those that a mesh axis runs over, the one named last changes fastest.
Arguments:
- tiles: float32 [2, 4608, 9216], P(None, 'row', 'col'), may hold values from -5 to 5
- pupils: float32 [2, 1024, 2048], P(None, 'row', 'col'), may hold values from -5 to 5
- intensity: float32 [16, 1024, 2048], P(None, 'row', 'col'), may hold values from 0.2 to 3
- offsets: int32 [8, 16, 2, 16], P('row', 'col'), may hold values from 0 to 448
Outputs:
- refocused: float32 [2, 4096, 8192], P(None, 'row', 'col')
Inputs may be any that keep to these rules, and one draw needn't show every extreme that they name: `offsets`: each window lies inside the tile's spectrum.
All inputs are finite; a program needn't handle non-finite values.
Results may differ from a plain program's by a relative error of at most 0.00017.
Values sent between devices are 32-bit elements; how exact they have to be, the bound alone decides.
A program may use at most 128 MiB of HBM per device.

v0:
```python
import math

import jax
import jax.numpy as jnp
from jax import lax
from jax.sharding import PartitionSpec as P

OVL = 64


STEP_SIZE = 0.05
TWO_PI = 2.0 * math.pi


def from_behind(value, axis, steps):
    count = lax.axis_size(axis)
    pairs = [(source, (source + steps) % count) for source in range(count)]
    return lax.ppermute(value, axis, pairs)


def propagator(rows, cols, total_rows, total_cols, fresnel):
    signed_rows = jnp.where(rows < total_rows // 2, rows, rows - total_rows)
    signed_cols = jnp.where(cols < total_cols // 2, cols, cols - total_cols)
    square_rows = (signed_rows * signed_rows).astype(jnp.float32)
    square_cols = (signed_cols * signed_cols).astype(jnp.float32)
    turns_rows = square_rows * (fresnel / (total_rows * total_rows))
    turns_rows = turns_rows - jnp.floor(turns_rows)
    turns_cols = square_cols * (fresnel / (total_cols * total_cols))
    turns_cols = turns_cols - jnp.floor(turns_cols)
    angle = -TWO_PI * (turns_rows[:, None] + turns_cols[None, :])
    decay = jnp.exp(
        -2.0
        * (
            square_rows[:, None] / (total_rows * total_rows)
            + square_cols[None, :] / (total_cols * total_cols)
        )
    )
    return (decay * jnp.cos(angle), decay * jnp.sin(angle))


def dft_table(length, sign, scale):
    index = jnp.arange(length, dtype=jnp.int32)
    product = index[:, None] * index[None, :] % length
    angle = product.astype(jnp.float32) * (TWO_PI / length)
    return (jnp.cos(angle) * scale, sign * scale * jnp.sin(angle))


def complex_apply(form, matrix_real, matrix_imag, value_real, value_imag):

    def product(left, right):
        return jnp.einsum(form, left, right, precision=lax.Precision.HIGHEST)

    out_real = product(matrix_real, value_real) - product(matrix_imag, value_imag)
    out_imag = product(matrix_real, value_imag) + product(matrix_imag, value_real)
    return (out_real, out_imag)


def complex_mul(left_real, left_imag, right_real, right_imag):
    return (
        left_real * right_real - left_imag * right_imag,
        left_real * right_imag + left_imag * right_real,
    )


def forward_pass(field, axis_dim, count, position, swapper):
    size = field.shape[1]
    segment = size // count
    length = size * count
    small_real, small_imag = dft_table(count, -1.0, 1.0)
    big_real, big_imag = dft_table(size, -1.0, 1.0)
    freq_low = jnp.arange(count, dtype=jnp.int32)[:, None]
    place_high = position * segment + jnp.arange(segment, dtype=jnp.int32)[None, :]
    turn_angle = (freq_low * place_high % length).astype(jnp.float32) * (-TWO_PI / length)
    turn_real, turn_imag = (jnp.cos(turn_angle), jnp.sin(turn_angle))
    mixed = swapper(field)
    if axis_dim == 1:
        block_real = mixed[0].reshape(count, segment, size)
        block_imag = mixed[1].reshape(count, segment, size)
        block_real, block_imag = complex_apply(
            "kp,psj->ksj", small_real, small_imag, block_real, block_imag
        )
        block_real, block_imag = complex_mul(
            block_real, block_imag, turn_real[:, :, None], turn_imag[:, :, None]
        )
        joined = swapper(jnp.stack([block_real, block_imag]).reshape(2, size, size))
        out_real, out_imag = complex_apply("ks,sj->kj", big_real, big_imag, joined[0], joined[1])
    else:
        block_real = mixed[0].reshape(size, count, segment)
        block_imag = mixed[1].reshape(size, count, segment)
        block_real, block_imag = complex_apply(
            "kp,jps->jks", small_real, small_imag, block_real, block_imag
        )
        block_real, block_imag = complex_mul(
            block_real, block_imag, turn_real[None], turn_imag[None]
        )
        joined = swapper(jnp.stack([block_real, block_imag]).reshape(2, size, size))
        out_real, out_imag = complex_apply("ks,js->jk", big_real, big_imag, joined[0], joined[1])
    return jnp.stack([out_real, out_imag])


def inverse_pass(field, axis_dim, count, position, swapper):
    size = field.shape[1]
    segment = size // count
    length = size * count
    small_real, small_imag = dft_table(count, 1.0, 1.0 / length)
    big_real, big_imag = dft_table(size, 1.0, 1.0)
    places = jnp.arange(size, dtype=jnp.int32)
    turn_angle = (places * position % length).astype(jnp.float32) * (TWO_PI / length)
    turn_real, turn_imag = (jnp.cos(turn_angle), jnp.sin(turn_angle))
    if axis_dim == 1:
        local_real, local_imag = complex_apply("sk,kj->sj", big_real, big_imag, field[0], field[1])
        local_real, local_imag = complex_mul(
            local_real, local_imag, turn_real[:, None], turn_imag[:, None]
        )
        joined = swapper(jnp.stack([local_real, local_imag]))
        block_real = joined[0].reshape(count, segment, size)
        block_imag = joined[1].reshape(count, segment, size)
        block_real, block_imag = complex_apply(
            "pk,ksj->psj", small_real, small_imag, block_real, block_imag
        )
    else:
        local_real, local_imag = complex_apply("sk,jk->js", big_real, big_imag, field[0], field[1])
        local_real, local_imag = complex_mul(
            local_real, local_imag, turn_real[None, :], turn_imag[None, :]
        )
        joined = swapper(jnp.stack([local_real, local_imag]))
        block_real = joined[0].reshape(size, count, segment)
        block_imag = joined[1].reshape(size, count, segment)
        block_real, block_imag = complex_apply(
            "pk,jks->jps", small_real, small_imag, block_real, block_imag
        )
    return swapper(jnp.stack([block_real, block_imag]).reshape(2, size, size))


def to_blocks(field, axis_dim, count, swapper):
    size = field.shape[1]
    segment = size // count
    mixed = swapper(field)
    if axis_dim == 1:
        return mixed.reshape(2, count, segment, size).transpose(0, 2, 1, 3).reshape(2, size, size)
    return mixed.reshape(2, size, count, segment).transpose(0, 1, 3, 2).reshape(2, size, size)


def from_blocks(field, axis_dim, count, swapper):
    size = field.shape[1]
    segment = size // count
    if axis_dim == 1:
        ordered = (
            field.reshape(2, segment, count, size).transpose(0, 2, 1, 3).reshape(2, size, size)
        )
    else:
        ordered = (
            field.reshape(2, size, segment, count).transpose(0, 1, 3, 2).reshape(2, size, size)
        )
    return swapper(ordered)


def row_swap(values):
    return lax.all_to_all(values, "row", split_axis=1, concat_axis=1, tiled=True)


def column_swap(values):
    return lax.all_to_all(values, "col", split_axis=2, concat_axis=2, tiled=True)


def local(tiles, pupils, intensity, offsets):
    tile_len = tiles.shape[1]
    window = pupils.shape[1]
    margin = OVL
    stride = tile_len - margin
    led_count = intensity.shape[0]
    tile_real, tile_imag = dft_table(tile_len, -1.0, 1.0 / math.sqrt(tile_len))
    spec_real, spec_imag = complex_apply("jk,kl->jl", tile_real, tile_imag, tiles[0], tiles[1])
    spec_real, spec_imag = complex_apply("lk,jk->jl", tile_real, tile_imag, spec_real, spec_imag)
    spectrum = jnp.stack([spec_real, spec_imag])
    starts = offsets[0, 0]

    def cut(row_start, col_start):
        return lax.dynamic_slice(
            spectrum, (jnp.int32(0), row_start, col_start), (2, window, window)
        )

    crops = jax.vmap(cut)(starts[0], starts[1])
    win_real, win_imag = dft_table(window, -1.0, 1.0 / math.sqrt(window))
    lens_real, lens_imag = (pupils[0], pupils[1])
    wave_real, wave_imag = complex_mul(lens_real, lens_imag, crops[:, 0], crops[:, 1])
    wave_real, wave_imag = complex_apply("jk,nkl->njl", win_real, -win_imag, wave_real, wave_imag)
    wave_real, wave_imag = complex_apply("lk,njk->njl", win_real, -win_imag, wave_real, wave_imag)
    excess = wave_real * wave_real + wave_imag * wave_imag - intensity
    grad_real, grad_imag = complex_apply(
        "jk,nkl->njl", win_real, win_imag, wave_real * excess, wave_imag * excess
    )
    grad_real, grad_imag = complex_apply("lk,njk->njl", win_real, win_imag, grad_real, grad_imag)
    update_real = lens_real * grad_real + lens_imag * grad_imag
    update_imag = lens_real * grad_imag - lens_imag * grad_real
    updates = jnp.stack([update_real, update_imag], axis=1)

    def place(led, total):
        corner = (jnp.int32(0), starts[0, led], starts[1, led])
        current = lax.dynamic_slice(total, corner, (2, window, window))
        return lax.dynamic_update_slice(total, current + updates[led], corner)

    total = lax.fori_loop(0, led_count, place, jnp.zeros_like(spectrum))
    new_spec = spectrum - STEP_SIZE * total
    obj_real, obj_imag = complex_apply("jk,kl->jl", tile_real, -tile_imag, new_spec[0], new_spec[1])
    obj_real, obj_imag = complex_apply("lk,jk->jl", tile_real, -tile_imag, obj_real, obj_imag)
    refined = jnp.stack([obj_real, obj_imag])
    ramp = (jnp.arange(margin, dtype=jnp.float32) + 0.5) / margin
    lower = from_behind(refined[:, stride:, :], "row", 1)
    top = ramp[:, None] * refined[:, :margin, :] + (1.0 - ramp)[:, None] * lower
    rowed = jnp.concatenate([top, refined[:, margin:stride, :]], axis=1)
    packed = rowed[:, :, stride:].reshape(2, stride * margin // 128, 128)
    left = from_behind(packed, "col", 1).reshape(2, stride, margin)
    front = ramp * rowed[:, :, :margin] + (1.0 - ramp) * left
    field = jnp.concatenate([front, rowed[:, :, margin:stride]], axis=2)
    row_count = lax.axis_size("row")
    col_count = lax.axis_size("col")
    row_place = lax.axis_index("row")
    col_place = lax.axis_index("col")
    fresnel = stride * row_count // 2
    local_index = jnp.arange(stride, dtype=jnp.int32)
    field = forward_pass(field, 1, row_count, row_place, row_swap)
    field = to_blocks(field, 1, row_count, row_swap)
    field = forward_pass(field, 2, col_count, col_place, column_swap)
    field = to_blocks(field, 2, col_count, column_swap)
    freq_rows = row_place * stride + local_index
    freq_cols = col_place * stride + local_index
    prop_real, prop_imag = propagator(
        freq_rows, freq_cols, stride * row_count, stride * col_count, fresnel
    )
    shifted_real, shifted_imag = complex_mul(field[0], field[1], prop_real, prop_imag)
    field = jnp.stack([shifted_real, shifted_imag])
    field = from_blocks(field, 2, col_count, column_swap)
    field = inverse_pass(field, 2, col_count, col_place, column_swap)
    field = from_blocks(field, 1, row_count, row_swap)
    field = inverse_pass(field, 1, row_count, row_place, row_swap)
    return field


def solution(mesh):
    placed = (
        P(None, "row", "col"),
        P(None, "row", "col"),
        P(None, "row", "col"),
        P("row", "col", None, None),
    )
    return jax.shard_map(
        local, mesh=mesh, in_specs=placed, out_specs=P(None, "row", "col"), check_vma=False
    )
```

profile of v0, /device:TPU:1, one launch (start us, length us, event | category | flops | bytes accessed | tf_op | source)
XLA Modules:
  0.0 971.7 jit_solution(15080167303509399332)
XLA Ops:
  0.0 12.2 %fusion.3 = f32[576,576]{1,0:T(8,128)} fusion(f32[2,576,576]{2,1,0:T(8,128)} %param.6), kind=kOutput, calls=%fused_computation.30 | convolution fusion | flops 2296553472 | bytes 2801664 | tf_op jit(solution)/shard_map/jk,kl->jl/dot_general | solution.py:51
  12.2 11.0 %fusion.5 = f32[576,576]{1,0:T(8,128)} fusion(f32[2,576,576]{2,1,0:T(8,128)S(1)} %copy-done.4), kind=kOutput, calls=%fused_computation.32 | convolution fusion | flops 2296553472 | bytes 2801664 | tf_op jit(solution)/shard_map/jk,kl->jl/dot_general | solution.py:51
  23.2 11.8 %fusion.17 = f32[576,576]{1,0:T(8,128)S(1)} fusion(f32[576,576]{1,0:T(8,128)} %fusion.3, f32[2,576,576]{2,1,0:T(8,128)} %param.6), kind=kOutput, calls=%fused_computation.49 | convolution fusion | flops 2296885248 | bytes 4276224 | tf_op jit(solution)/shard_map/jk,kl->jl/dot_general | solution.py:51
  35.0 10.1 %fusion.41 = f32[576,576]{1,0:T(8,128)S(1)} fusion(f32[576,576]{1,0:T(8,128)S(1)} %fusion.17), kind=kOutput, calls=%fused_computation.97 | convolution fusion | flops 2296553472 | bytes 2654208 | tf_op jit(solution)/shard_map/lk,jk->jl/dot_general | solution.py:51
  45.1 9.9 %fusion.14 = f32[576,576]{1,0:T(8,128)S(1)} fusion(f32[576,576]{1,0:T(8,128)S(1)} %copy-done.6, f32[2,576,576]{2,1,0:T(8,128)S(1)} %copy-done.5), kind=kOutput, calls=%fused_computation.48 | convolution fusion | flops 2296885248 | bytes 4276224 | tf_op jit(solution)/shard_map/jk,kl->jl/dot_general | solution.py:51
  55.0 9.6 fusion.42
  64.7 11.2 %add_bitcast_fusion.1 = f32[1,576,576]{2,1,0:T(8,128)} fusion(f32[576,576]{1,0:T(8,128)S(1)} %fusion.41, f32[576,576]{1,0:T(8,128)S(1)} %fusion.14), kind=kOutput, calls=%fused_computation.40 | convolution fusion | flops 2296885248 | bytes 3981312 | tf_op jit(solution)/shard_map/lk,jk->jl/dot_general | solution.py:51
  75.9 11.0 %subtract_bitcast_fusion.1 = f32[1,576,576]{2,1,0:T(8,128)} fusion(f32[576,576]{1,0:T(8,128)S(1)} %fusion.42, f32[576,576]{1,0:T(8,128)S(1)} %fusion.17), kind=kOutput, calls=%fused_computation.41 | convolution fusion | flops 2296885248 | bytes 3981312 | tf_op jit(solution)/shard_map/lk,jk->jl/dot_general | solution.py:51
  86.9 3.6 pad_maximum_fusion
  90.5 47.9 %while.15 = (s32[]{:T(128)}, f32[2,576,576]{2,1,0:T(8,128)}, s32[16,3]{0,1:T(4,128)S(1)}, f32[16,2,128,128]{3,2,0,1:T(8,128)S(1)}, s32[]{:T(128)}) while((s32[]{:T(128)}, f32[2,576,576]{2,1,0:T(8,128)}, s32[16,3]{0,1:T(4,128)S(1)}, f32[16,2,128,128]{3,2,0,1:T(8,128)S(1)}, s32[]{:T(128)}) %tuple.74), condition=%wide.while_cond, body=%wide.while_body.sunk | while | flops 2 | bytes 262261 | solution.py:179
  154.6 3.1 fusion.236
  157.7 3.0 fusion.232
  160.7 3.4 fusion.35
  176.1 125.1 %while.14 = (s32[]{:T(128)}, f32[2,576,576]{2,1,0:T(8,128)S(1)}, s32[2,16]{1,0:T(2,128)S(1)}, f32[16,2,128,128]{3,2,0,1:T(8,128)}, s32[]{:T(128)}, /*index=5*/s32[]{:T(128)}, s32[]{:T(128)}) while((s32[]{:T(128)}, f32[2,576,576]{2,1,0:T(8,128)S(1)}, s32[2,16]{1,0:T(2,128)S(1)}, f32[16,2,128,128]{3,2,0,1:T(8,128)}, s32[]{:T(128)}, ...), condition=%wide.region_1.2_spmd, body=%wide.region_0.1_spmd.sunk | while | flops 32776 | bytes 655541 | solution.py:203
  189.0 2.5 dynamic_update_slice.8
  303.3 9.7 fusion.20
  313.0 10.1 %fusion.21 = f32[576,576]{1,0:T(8,128)S(1)} fusion(f32[2,576,576]{2,1,0:T(8,128)S(1)} %multiply_subtract_fusion), kind=kOutput, calls=%fused_computation.53 | convolution fusion | flops 2296553472 | bytes 2801664 | tf_op jit(solution)/shard_map/jk,kl->jl/dot_general | solution.py:51
  323.2 9.9 %convolution_subtract_fusion = f32[576,576]{1,0:T(8,128)S(1)} fusion(f32[576,576]{1,0:T(8,128)S(1)} %fusion.20, f32[2,576,576]{2,1,0:T(8,128)S(1)} %multiply_subtract_fusion), kind=kOutput, calls=%fused_computation.51 | convolution fusion | flops 2297217024 | bytes 4276224 | tf_op jit(solution)/shard_map/jk,kl->jl/dot_general | solution.py:51
  333.1 9.9 %fusion.40 = f32[576,576]{1,0:T(8,128)S(1)} fusion(f32[576,576]{1,0:T(8,128)S(1)} %convolution_subtract_fusion), kind=kOutput, calls=%fused_computation.96 | convolution fusion | flops 2296553472 | bytes 2654208 | tf_op jit(solution)/shard_map/lk,jk->jl/dot_general | solution.py:51
  343.0 10.2 %convolution_add_fusion = f32[576,576]{1,0:T(8,128)S(1)} fusion(f32[576,576]{1,0:T(8,128)S(1)} %fusion.21, f32[2,576,576]{2,1,0:T(8,128)S(1)} %multiply_subtract_fusion), kind=kOutput, calls=%fused_computation.50 | convolution fusion | flops 2297217024 | bytes 4276224 | tf_op jit(solution)/shard_map/jk,kl->jl/dot_general | solution.py:51
  353.2 9.6 fusion.39
  362.8 9.9 %subtract_bitcast_fusion = f32[1,576,576]{2,1,0:T(8,128)S(1)} fusion(f32[576,576]{1,0:T(8,128)S(1)} %fusion.40, f32[576,576]{1,0:T(8,128)S(1)} %convolution_add_fusion), kind=kOutput, calls=%fused_computation.39 | convolution fusion | flops 2297217024 | bytes 3981312 | tf_op jit(solution)/shard_map/lk,jk->jl/dot_general | solution.py:51
  372.7 10.0 %add_bitcast_fusion = f32[1,576,576]{2,1,0:T(8,128)S(1)} fusion(f32[576,576]{1,0:T(8,128)S(1)} %fusion.39, f32[576,576]{1,0:T(8,128)S(1)} %convolution_subtract_fusion), kind=kOutput, calls=%fused_computation.38 | convolution fusion | flops 2297217024 | bytes 3981312 | tf_op jit(solution)/shard_map/lk,jk->jl/dot_general | solution.py:51
  382.7 2.7 collective-permute-start
  385.4 12.6 %collective-permute-done = f32[2,64,576]{2,1,0:T(8,128)S(1)} collective-permute-done((f32[2,64,576]{2,1,0:T(8,128)S(1)}, f32[2,64,576]{2,1,0:T(8,128)S(1)}, u32[]{:S(2)}, u32[]{:S(2)}) %collective-permute-start) | collective-permute-done | bytes 294944 | tf_op jit(solution)/shard_map/ppermute | solution.py:18
  406.1 2.9 copy.280
  409.0 4.0 all-to-all-start
  413.3 21.2 %all-to-all-done = f32[2,512,512]{2,0,1:T(2,128)S(1)} async-done(((f32[2,512,512]{2,0,1:T(2,128)}), f32[2,512,512]{2,0,1:T(2,128)S(1)}, u32[]{:S(2)}, u32[]{:S(2)}) %all-to-all-start) | async-done | bytes 2097184 | tf_op jit(solution)/shard_map/all_to_all | solution.py:159
  445.7 36.3 %all_to_all.60 = f32[2,512,512]{2,0,1:T(2,128)S(1)} all-to-all(f32[2,512,512]{2,0,1:T(2,128)S(1)} %copy.291), channel_id=1, replica_groups=mesh['row'=8,'col'=16] {'row'}, dimensions={1} | all-to-all | bytes 4194304 | tf_op jit(solution)/shard_map/all_to_all | solution.py:159
  483.6 5.7 fusion.68
  489.3 6.1 fusion.64
  495.5 5.8 fusion.33
  501.2 5.9 fusion.32
  509.0 28.4 %all_to_all.61 = f32[2,512,512]{2,0,1:T(2,128)S(1)} all-to-all(f32[2,512,512]{2,0,1:T(2,128)S(1)} %copy.292), channel_id=1, replica_groups=mesh['row'=8,'col'=16] {'row'}, dimensions={1} | all-to-all | bytes 4194304 | tf_op jit(solution)/shard_map/all_to_all | solution.py:159
  541.5 10.2 %all-to-all-start.3 = ((f32[2,512,512]{1,0,2:T(2,128)}), f32[2,512,512]{1,0,2:T(2,128)S(1)}, u32[]{:S(2)}, u32[]{:S(2)}) async-start(f32[2,512,512]{1,0,2:T(2,128)} %copy.295), calls=%async_computation.3 | async-start | bytes 4194304 | tf_op jit(solution)/shard_map/all_to_all | solution.py:163
  551.8 27.0 %all-to-all-done.3 = f32[2,512,512]{1,0,2:T(2,128)S(1)} async-done(((f32[2,512,512]{1,0,2:T(2,128)}), f32[2,512,512]{1,0,2:T(2,128)S(1)}, u32[]{:S(2)}, u32[]{:S(2)}) %all-to-all-start.3) | async-done | bytes 2097184 | tf_op jit(solution)/shard_map/all_to_all | solution.py:163
  591.2 30.3 %all_to_all.62 = f32[2,512,512]{1,0,2:T(2,128)S(1)} all-to-all(f32[2,512,512]{1,0,2:T(2,128)S(1)} %copy.304), channel_id=1, replica_groups=mesh['row'=8,'col'=16] {'col'}, dimensions={2} | all-to-all | bytes 4194304 | tf_op jit(solution)/shard_map/all_to_all | solution.py:163
  623.2 7.1 fusion.62
  630.3 7.3 fusion.58
  637.6 7.2 fusion.29
  644.8 7.4 fusion.28
  654.8 4.7 all-to-all-start.5
  659.5 27.2 %all-to-all-done.5 = f32[2,512,512]{1,0,2:T(2,128)S(1)} async-done(((f32[2,512,512]{1,0,2:T(2,128)}), f32[2,512,512]{1,0,2:T(2,128)S(1)}, u32[]{:S(2)}, u32[]{:S(2)}) %all-to-all-start.5) | async-done | bytes 2097184 | tf_op jit(solution)/shard_map/all_to_all | solution.py:163
  687.0 4.5 multiply_subtract_fusion.1
  691.8 2.9 copy.307
  694.8 4.8 all-to-all-start.6
  699.6 26.8 %all-to-all-done.6 = f32[2,512,512]{1,0,2:T(2,128)S(1)} async-done(((f32[2,512,512]{1,0,2:T(2,128)}), f32[2,512,512]{1,0,2:T(2,128)S(1)}, u32[]{:S(2)}, u32[]{:S(2)}) %all-to-all-start.6) | async-done | bytes 2097184 | tf_op jit(solution)/shard_map/all_to_all | solution.py:163
  728.0 7.1 fusion.52
  735.1 7.3 fusion.56
  742.4 7.1 convolution_add_fusion.4
  749.5 7.5 subtract_bitcast_fusion.3
  759.6 31.5 %all_to_all.63 = f32[2,512,512]{1,0,2:T(2,128)S(1)} all-to-all(f32[2,512,512]{1,0,2:T(2,128)} %copy.308), channel_id=1, replica_groups=mesh['row'=8,'col'=16] {'col'}, dimensions={2} | all-to-all | bytes 4194304 | tf_op jit(solution)/shard_map/all_to_all | solution.py:163
  802.8 30.4 %all_to_all.64 = f32[2,512,512]{1,0,2:T(2,128)S(1)} all-to-all(f32[2,512,512]{1,0,2:T(2,128)S(1)} %copy.317), channel_id=1, replica_groups=mesh['row'=8,'col'=16] {'col'}, dimensions={2} | all-to-all | bytes 4194304 | tf_op jit(solution)/shard_map/all_to_all | solution.py:163
  833.1 2.8 copy.318
  835.9 2.8 copy.319
  838.7 2.9 copy.320
  841.6 3.8 all-to-all-start.9
  845.5 25.8 %all-to-all-done.9 = f32[2,512,512]{2,0,1:T(2,128)S(1)} async-done(((f32[2,512,512]{2,0,1:T(2,128)}), f32[2,512,512]{2,0,1:T(2,128)S(1)}, u32[]{:S(2)}, u32[]{:S(2)}) %all-to-all-start.9) | async-done | bytes 2097184 | tf_op jit(solution)/shard_map/all_to_all | solution.py:159
  872.9 5.7 fusion.46
  878.6 6.1 fusion.50
  884.7 5.8 convolution_add_fusion.2
  890.5 6.1 subtract_bitcast_fusion.2
  898.5 31.9 %all_to_all.65 = f32[2,512,512]{2,0,1:T(2,128)S(1)} all-to-all(f32[2,512,512]{2,0,1:T(2,128)S(1)} %copy.321), channel_id=1, replica_groups=mesh['row'=8,'col'=16] {'row'}, dimensions={1} | all-to-all | bytes 4194304 | tf_op jit(solution)/shard_map/all_to_all | solution.py:159
  941.2 28.6 %all_to_all.66 = f32[2,512,512]{2,0,1:T(2,128)S(1)} all-to-all(f32[2,512,512]{2,0,1:T(2,128)S(1)} %copy.330), channel_id=1, replica_groups=mesh['row'=8,'col'=16] {'row'}, dimensions={1} | all-to-all | bytes 4194304 | tf_op jit(solution)/shard_map/all_to_all | solution.py:159
  (214 shorter events, 217.1 us)
Async XLA Ops:
  0.0 12.2 %copy-start.4 = (f32[2,576,576]{2,1,0:T(8,128)S(1)}, f32[2,576,576]{2,1,0:T(8,128)}, u32[]{:S(2)}) copy-start(f32[2,576,576]{2,1,0:T(8,128)} %param.6) | copy-start | bytes 7962628
  35.0 10.1 %copy-start.5 = (f32[2,576,576]{2,1,0:T(8,128)S(1)}, f32[2,576,576]{2,1,0:T(8,128)}, u32[]{:S(2)}) copy-start(f32[2,576,576]{2,1,0:T(8,128)} %param.6) | copy-start | bytes 7962628
  35.0 10.1 %copy-start.6 = (f32[576,576]{1,0:T(8,128)S(1)}, f32[576,576]{1,0:T(8,128)}, u32[]{:S(2)}) copy-start(f32[576,576]{1,0:T(8,128)} %fusion.5) | copy-start | bytes 3981316
  75.9 11.0 %copy-start.3 = (s32[1,1,2,16]{3,2,1,0:T(2,128)S(1)}, s32[1,1,2,16]{3,2,1,0:T(2,128)}, u32[]{:S(2)}) copy-start(s32[1,1,2,16]{3,2,1,0:T(2,128)} %param.9) | copy-start | bytes 388
  90.5 47.9 %copy-start.2 = (f32[2,128,128]{2,1,0:T(8,128)S(1)}, f32[2,128,128]{2,1,0:T(8,128)}, u32[]{:S(2)}) copy-start(f32[2,128,128]{2,1,0:T(8,128)} %param.7) | copy-start | bytes 393220
  152.7 1.9 copy-start
  160.7 3.4 copy-start.1
  382.7 15.3 %collective-permute-start = (f32[2,64,576]{2,1,0:T(8,128)S(1)}, f32[2,64,576]{2,1,0:T(8,128)S(1)}, u32[]{:S(2)}, u32[]{:S(2)}) collective-permute-start(f32[2,64,576]{2,1,0:T(8,128)S(1)} %pad_maximum_fusion.12), channel_id=1, source_target_pairs={{0,16},{16,32},{32,48},{48,64},{64,80},{80,96},{96,112},{112,0},{1... | collective-permute-start | bytes 884744 | tf_op jit(solution)/shard_map/ppermute | solution.py:18
  398.5 4.2 collective-permute-start.1
  409.0 25.5 %all-to-all-start = ((f32[2,512,512]{2,0,1:T(2,128)}), f32[2,512,512]{2,0,1:T(2,128)S(1)}, u32[]{:S(2)}, u32[]{:S(2)}) async-start(f32[2,512,512]{2,0,1:T(2,128)} %copy.280), calls=%async_computation | async-start | bytes 4194304 | tf_op jit(solution)/shard_map/all_to_all | solution.py:159
  541.5 37.3 %all-to-all-start.3 = ((f32[2,512,512]{1,0,2:T(2,128)}), f32[2,512,512]{1,0,2:T(2,128)S(1)}, u32[]{:S(2)}, u32[]{:S(2)}) async-start(f32[2,512,512]{1,0,2:T(2,128)} %copy.295), calls=%async_computation.3 | async-start | bytes 4194304 | tf_op jit(solution)/shard_map/all_to_all | solution.py:163
  654.8 31.9 %all-to-all-start.5 = ((f32[2,512,512]{1,0,2:T(2,128)}), f32[2,512,512]{1,0,2:T(2,128)S(1)}, u32[]{:S(2)}, u32[]{:S(2)}) async-start(f32[2,512,512]{1,0,2:T(2,128)} %copy.305), calls=%async_computation.5 | async-start | bytes 4194304 | tf_op jit(solution)/shard_map/all_to_all | solution.py:163
  694.8 31.6 %all-to-all-start.6 = ((f32[2,512,512]{1,0,2:T(2,128)}), f32[2,512,512]{1,0,2:T(2,128)S(1)}, u32[]{:S(2)}, u32[]{:S(2)}) async-start(f32[2,512,512]{1,0,2:T(2,128)} %copy.307), calls=%async_computation.6 | async-start | bytes 4194304 | tf_op jit(solution)/shard_map/all_to_all | solution.py:163
  841.6 29.7 %all-to-all-start.9 = ((f32[2,512,512]{2,0,1:T(2,128)}), f32[2,512,512]{2,0,1:T(2,128)S(1)}, u32[]{:S(2)}, u32[]{:S(2)}) async-start(f32[2,512,512]{2,0,1:T(2,128)} %copy.320), calls=%async_computation.9 | async-start | bytes 4194304 | tf_op jit(solution)/shard_map/all_to_all | solution.py:159
where the time goes:
time: 987 us; the launch traced here: 972 us
  matrix products  333 us (34%)
  blocking collectives  217 us (22%)
  local copies, waits for them, and re-layouts  155 us (16%)
  waiting for transfers between devices  142 us (14%)
  loops' own time  59.6 us (6%)
  other arithmetic  32.7 us (3%)
  starting transfers between devices  31 us (3%)
    dot_general x64, matrix products, product(): return jnp.einsum(form, left, right, precision=lax.Precision.HIGHEST)  333 us
    all_to_all x4, blocking collectives, row_swap(): lax.all_to_all(values, 'row', split_axis=1, concat_axis=1, tiled=True)  125 us
    all_to_all x3, blocking collectives, column_swap(): lax.all_to_all(values, 'col', split_axis=2, concat_axis=2, tiled=True)  92.2 us
    all_to_all x3, waiting for transfers between devices, column_swap(): lax.all_to_all(values, 'col', split_axis=2, concat_axis=2, tiled=True)  80.9 us
    another operation x1, loops' own time, local(): total = lax.fori_loop(0, led_count, place, jnp.zeros_like(spectrum))  59.4 us
    gather x48, local copies, waits for them, and re-layouts  47.6 us
    all_to_all x2, waiting for transfers between devices, row_swap(): lax.all_to_all(values, 'row', split_axis=1, concat_axis=1, tiled=True)  47 us
    dynamic_update_slice x16, local copies, waits for them, and re-layouts, place(): return lax.dynamic_update_slice(total, current + updates[led], corner)  39 us
  transfers between devices with their start and end apart: 7, of which 7 were waited for; matrix products, arithmetic and copies ran while one was open for 0% of the time, Pallas kernels for 0%

commit v1 on v0

v1 whole, which is shorter than its diff:
```python
import math

import numpy as np
import ml_dtypes
import jax
import jax.numpy as jnp
from jax import lax
from jax.experimental import pallas as pl
from jax.experimental.pallas import tpu as pltpu
from jax.sharding import PartitionSpec as P

TILE = 576
PAD = 640
OVL = 64
WIN = 128
LEDS = 16
STRIDE = 512
ROWS = 4096
COLS = 8192
FRESNEL = 2048
STEP_SIZE = 0.05
RADIX = 6
SUB = TILE // RADIX
BF = jnp.bfloat16
F32 = jnp.float32
GROUP = 4


def split_np(table):
    table = np.asarray(table, np.float64)
    high = table.astype(np.float32).astype(ml_dtypes.bfloat16)
    low = (table - high.astype(np.float64)).astype(np.float32).astype(ml_dtypes.bfloat16)
    return high, low


def unit(turns):
    turns = np.asarray(turns, np.float64)
    return np.exp(2j * np.pi * (turns - np.floor(turns)))


def right_block(table):
    return np.block([[table.real, table.imag], [-table.imag, table.real]])


def left_block(table):
    return np.block([[table.real, -table.imag], [table.imag, table.real]])


def dft_np(length, sign):
    index = np.arange(length)
    return unit(sign * (index[:, None] * index[None, :] % length) / length)


def axis_filter(length):
    freq = np.arange(length)
    signed = np.where(freq < length // 2, freq, freq - length).astype(np.float64)
    turns = signed * signed * (FRESNEL / (length * length))
    return np.exp(-2.0 * signed * signed / (length * length)) * unit(-turns) / length


def split(value):
    high = value.astype(BF)
    low = (value - high.astype(F32)).astype(BF)
    return high, low


def mm(left, right):
    return jnp.dot(left, right, preferred_element_type=F32)


def mm3(left, right):
    return mm(left[0], right[0]) + (mm(left[1], right[0]) + mm(left[0], right[1]))


def mm_nt(left, right):
    return lax.dot_general(left, right, (((1,), (1,)), ((), ())), preferred_element_type=F32)


def cmul(ar, ai, br, bi):
    return ar * br - ai * bi, ar * bi + ai * br


def cscale(value, factor):
    re, im = value
    fr, fi = float(factor.real), float(factor.imag)
    near = 1e-12
    if abs(fi) < near:
        if abs(fr - 1) < near:
            return re, im
        if abs(fr + 1) < near:
            return -re, -im
    if abs(fr) < near:
        if abs(fi - 1) < near:
            return -im, re
        if abs(fi + 1) < near:
            return im, -re
    if abs(abs(fr) - abs(fi)) < near:
        size = abs(fr)
        sr, si = math.copysign(1, fr), math.copysign(1, fi)
        left = re if sr > 0 else -re
        low = im if sr > 0 else -im
        new_re = left - im if si > 0 else left + im
        new_im = low + re if si > 0 else low - re
        return new_re * size, new_im * size
    return re * fr - im * fi, re * fi + im * fr


def fft_list(items, sign):
    count = len(items)
    if count == 1:
        return items
    if count == 3:
        (ar, ai), (br, bi), (cr, ci) = items
        sr, si, dr, di = br + cr, bi + ci, br - cr, bi - ci
        mr, mi = ar - 0.5 * sr, ai - 0.5 * si
        root = sign * math.sqrt(0.75)
        tr, ti = -root * di, root * dr
        return [(ar + sr, ai + si), (mr + tr, mi + ti), (mr - tr, mi - ti)]
    even = fft_list(items[0::2], sign)
    odd = fft_list(items[1::2], sign)
    half = count // 2
    first, second = [], []
    for index in range(half):
        turned = cscale(odd[index], unit(sign * index / count))
        er, ei = even[index]
        first.append((er + turned[0], ei + turned[1]))
        second.append((er - turned[0], ei - turned[1]))
    return first + second


def tile_tables():
    index = np.arange(TILE)
    low = unit(-(np.arange(24)[:, None] * index[None, :] % TILE) / TILE) / math.sqrt(TILE)
    high = unit(-(24 * np.arange(24)[:, None] * index[None, :] % TILE) / TILE)
    seeds = np.zeros((4, 24, PAD), np.float32)
    seeds[0, :, :TILE], seeds[1, :, :TILE] = low.real, low.imag
    seeds[2, :, :TILE], seeds[3, :, :TILE] = high.real, high.imag
    small = np.arange(SUB)
    forward, inverse = [], []
    for part in range(RADIX):
        turned = unit(-(part * small[:, None] + RADIX * small[:, None] * small[None, :]) / TILE)
        turned = turned / math.sqrt(TILE)
        forward.append(left_block(turned))
        inverse.append(left_block(np.conj(turned.T)))
    forward = np.stack(split_np(np.stack(forward)))
    inverse = np.stack(split_np(np.stack(inverse)))
    window = dft_np(WIN, -1) / math.sqrt(WIN)
    lanes = np.stack(
        [*split_np(right_block(np.conj(window))), *split_np(right_block(window))]
    )
    sides = np.stack(
        [*split_np(left_block(np.conj(window))), *split_np(left_block(window))]
    )
    return seeds, forward, inverse, lanes, sides


def cut(ref, part, row, first, back):
    base = pl.multiple_of((row // 8) * 8, 8)
    down = row - base
    wide = ref[part, pl.ds(base, WIN + 8), pl.ds(first, 256)]
    wide = pltpu.roll(wide, back, 1)[:, :WIN].reshape(WIN // 8 + 1, 8, WIN)
    wide = pltpu.roll(wide, lax.rem(8 - down, 8), 1)
    lane = lax.broadcasted_iota(jnp.int32, (WIN // 8, 8, WIN), 1)
    return jnp.where(lane < 8 - down, wide[:-1], wide[1:]).reshape(WIN, WIN)


def add(ref, part, row, first, shift, value):
    base = pl.multiple_of((row // 8) * 8, 8)
    down = row - base
    turned = pltpu.roll(value.reshape(WIN // 8, 8, WIN), down, 1)
    zero = jnp.zeros((1, 8, WIN), F32)
    lane = lax.broadcasted_iota(jnp.int32, (WIN // 8 + 1, 8, WIN), 1)
    upper = jnp.concatenate([zero, turned], axis=0)
    lower = jnp.concatenate([turned, zero], axis=0)
    tall = jnp.where(lane < down, upper, lower).reshape(WIN + 8, WIN)
    wide = jnp.concatenate([tall, jnp.zeros((WIN + 8, 128), F32)], axis=1)
    here = (part, pl.ds(base, WIN + 8), pl.ds(first, 256))
    ref[here] = ref[here] + pltpu.roll(wide, shift, 1)


def tile_body(
    offs, tiles, pupils, intensity, seeds, fwd, inv, lanes, sides, out,
    base, t_hi, t_lo, l_hi, l_lo, x_hi, x_lo, y, sub, spec, new, v_hi, v_lo, win_a, win_b,
):
    low_r, low_i = seeds[0], seeds[1]

    @pl.loop(0, 24)
    def _(a):
        hr = seeds[2, pl.ds(a, 1), :]
        hi = seeds[3, pl.ds(a, 1), :]
        tr, ti = cmul(low_r, low_i, hr, hi)
        start = pl.multiple_of(a * 24, 8)
        base[0, pl.ds(start, 24), :] = tr
        base[1, pl.ds(start, 24), :] = ti

    zero_tail = jnp.zeros((PAD - TILE, 2 * PAD), BF)
    t_hi[TILE:PAD, :] = zero_tail
    t_lo[TILE:PAD, :] = zero_tail
    t_hi[PAD + TILE :, :] = zero_tail
    t_lo[PAD + TILE :, :] = zero_tail

    @pl.loop(0, TILE // 96)
    def _(a):
        start = pl.multiple_of(a * 96, 16)
        ch, cl = split(base[0, pl.ds(start, 96), :])
        sh, sl = split(base[1, pl.ds(start, 96), :])
        t_hi[pl.ds(start, 96), :PAD] = ch
        t_lo[pl.ds(start, 96), :PAD] = cl
        t_hi[pl.ds(start, 96), PAD:] = sh
        t_lo[pl.ds(start, 96), PAD:] = sl
        t_hi[pl.ds(start + PAD, 96), :PAD] = -sh
        t_lo[pl.ds(start + PAD, 96), :PAD] = -sl
        t_hi[pl.ds(start + PAD, 96), PAD:] = ch
        t_lo[pl.ds(start + PAD, 96), PAD:] = cl

    x_hi[...] = jnp.zeros_like(x_hi)
    x_lo[...] = jnp.zeros_like(x_lo)

    @pl.loop(0, TILE // 96)
    def _(a):
        start = pl.multiple_of(a * 96, 16)
        for part in range(2):
            high, low = split(tiles[part, pl.ds(start, 96), :])
            x_hi[pl.ds(start, 96), part * PAD : part * PAD + TILE] = high
            x_lo[pl.ds(start, 96), part * PAD : part * PAD + TILE] = low

    @pl.loop(0, 2 * PAD // 256)
    def _(n):
        at = pl.ds(pl.multiple_of(n * 256, 256), 256)
        both = mm3((x_hi[...], x_lo[...]), (t_hi[:, at], t_lo[:, at]))
        y[2 * n] = both[:, :128]
        y[2 * n + 1] = both[:, 128:]

    @pl.loop(0, RADIX)
    def _(b):
        rows = pl.ds(b, SUB, stride=RADIX)
        parts = [
            jnp.concatenate([y[n, rows, :] for n in range(5 * part, 5 * part + 5)], axis=1)
            for part in range(2)
        ]
        sub[b] = mm3((fwd[0, b], fwd[1, b]), split(jnp.concatenate(parts, axis=0)))

    @pl.loop(0, PAD // 128)
    def _(n):
        at = pl.ds(pl.multiple_of(n * 128, 128), 128)
        for row in range(0, SUB, 8):
            items = [
                (sub[b, row : row + 8, at], sub[b, SUB + row : SUB + row + 8, at])
                for b in range(RADIX)
            ]
            done = fft_list(items, -1)
            for k in range(RADIX):
                here = slice(k * SUB + row, k * SUB + row + 8)
                spec[0, here, at] = done[k][0]
                spec[1, here, at] = done[k][1]
                new[0, here, at] = done[k][0]
                new[1, here, at] = done[k][1]

    for ref in (spec, new):
        for part in range(2):
            ref[part, TILE:, :] = jnp.zeros((8, PAD), F32)
    pr, pi = pupils[0], pupils[1]
    inv_lanes = (lanes[0], lanes[1])
    fwd_lanes = (lanes[2], lanes[3])
    inv_sides = (sides[0], sides[1])
    fwd_sides = (sides[2], sides[3])

    @pl.loop(0, LEDS // GROUP)
    def _(step):
        for j in range(GROUP):
            led = step * GROUP + j
            row, col = offs[0, led], offs[1, led]
            first = pl.multiple_of((col // 128) * 128, 128)
            shift = col - first
            back = lax.rem(256 - shift, 256)
            cr = cut(spec, 0, row, first, back)
            ci = cut(spec, 1, row, first, back)
            wr, wi = cmul(pr, pi, cr, ci)
            win_a[:WIN, j * WIN : (j + 1) * WIN] = wr
            win_a[WIN:, j * WIN : (j + 1) * WIN] = wi
        side = mm3(inv_sides, split(win_a[...]))
        for j in range(GROUP):
            win_b[j * WIN : (j + 1) * WIN, :WIN] = side[:WIN, j * WIN : (j + 1) * WIN]
            win_b[j * WIN : (j + 1) * WIN, WIN:] = side[WIN:, j * WIN : (j + 1) * WIN]
        wave = mm3(split(win_b[...]), inv_lanes)
        for j in range(GROUP):
            wr = wave[j * WIN : (j + 1) * WIN, :WIN]
            wi = wave[j * WIN : (j + 1) * WIN, WIN:]
            excess = wr * wr + wi * wi - intensity[step * GROUP + j]
            win_b[j * WIN : (j + 1) * WIN, :WIN] = wr * excess
            win_b[j * WIN : (j + 1) * WIN, WIN:] = wi * excess
        grad = mm3(split(win_b[...]), fwd_lanes)
        for j in range(GROUP):
            win_a[:WIN, j * WIN : (j + 1) * WIN] = grad[j * WIN : (j + 1) * WIN, :WIN]
            win_a[WIN:, j * WIN : (j + 1) * WIN] = grad[j * WIN : (j + 1) * WIN, WIN:]
        win_a[...] = mm3(fwd_sides, split(win_a[...]))
        for j in range(GROUP):
            led = step * GROUP + j
            row, col = offs[0, led], offs[1, led]
            first = pl.multiple_of((col // 128) * 128, 128)
            shift = col - first
            gr = win_a[:WIN, j * WIN : (j + 1) * WIN] * -STEP_SIZE
            gi = win_a[WIN:, j * WIN : (j + 1) * WIN] * -STEP_SIZE
            ur, ui = cmul(pr, -pi, gr, gi)
            add(new, 0, row, first, shift, ur)
            add(new, 1, row, first, shift, ui)

    @pl.loop(0, PAD // 128)
    def _(n):
        at = pl.ds(pl.multiple_of(n * 128, 128), 128)
        for row in range(0, SUB, 8):
            items = []
            for k in range(RADIX):
                here = slice(k * SUB + row, k * SUB + row + 8)
                items.append((new[0, here, at], new[1, here, at]))
            done = fft_list(items, 1)
            for b in range(RADIX):
                sub[b, row : row + 8, at] = done[b][0]
                sub[b, SUB + row : SUB + row + 8, at] = done[b][1]

    @pl.loop(0, RADIX)
    def _(b):
        mixed = mm3((inv[0, b], inv[1, b]), split(sub[b]))
        rows = pl.ds(b, SUB, stride=RADIX)
        for n in range(5):
            y[n, rows, :] = mixed[:SUB, 128 * n : 128 * n + 128]
            y[5 + n, rows, :] = mixed[SUB:, 128 * n : 128 * n + 128]

    def put(start, count, real_at, imag_at):
        for n in range(5):
            rh, rl = split(y[n, start : start + count, :])
            ih, il = split(y[5 + n, start : start + count, :])
            left, right = slice(128 * n, 128 * n + 128), slice(PAD + 128 * n, PAD + 128 * n + 128)
            a = slice(real_at, real_at + count)
            v_hi[a, left], v_hi[a, right] = rh, ih
            v_lo[a, left], v_lo[a, right] = rl, il
            b = slice(imag_at, imag_at + count)
            v_hi[b, left], v_hi[b, right] = ih, -rh
            v_lo[b, left], v_lo[b, right] = il, -rl

    put(0, STRIDE, 0, STRIDE)
    put(STRIDE, OVL, 2 * STRIDE, 2 * STRIDE + OVL)

    for at, width in ((0, 256), (256, 256), (512, 256), (768, 256), (1024, 128)):
        right = (v_hi[at : at + width, :], v_lo[at : at + width, :])
        left = (t_hi[:TILE, :], t_lo[:TILE, :])
        out[:, at : at + width] = (
            mm_nt(left[0], right[0]) + (mm_nt(left[1], right[0]) + mm_nt(left[0], right[1]))
        )


def vmem():
    return pl.BlockSpec(memory_space=pltpu.VMEM)


def tile_step(tiles, pupils, intensity, offsets):
    seeds, fwd, inv, lanes, sides = tile_tables()
    return pl.pallas_call(
        tile_body,
        out_shape=jax.ShapeDtypeStruct((TILE, 2 * TILE), F32),
        in_specs=[pl.BlockSpec(memory_space=pltpu.SMEM)] + [vmem()] * 8,
        out_specs=vmem(),
        scratch_shapes=[
            pltpu.VMEM((2, TILE, PAD), F32),
            pltpu.VMEM((2 * PAD, 2 * PAD), BF),
            pltpu.VMEM((2 * PAD, 2 * PAD), BF),
            pltpu.VMEM((16, 128), BF),
            pltpu.VMEM((16, 128), BF),
            pltpu.VMEM((TILE, 2 * PAD), BF),
            pltpu.VMEM((TILE, 2 * PAD), BF),
            pltpu.VMEM((2 * PAD // 128, TILE, 128), F32),
            pltpu.VMEM((RADIX, 2 * SUB, PAD), F32),
            pltpu.VMEM((2, TILE + 8, PAD), F32),
            pltpu.VMEM((2, TILE + 8, PAD), F32),
            pltpu.VMEM((2 * TILE, 2 * PAD), BF),
            pltpu.VMEM((2 * TILE, 2 * PAD), BF),
            pltpu.VMEM((2 * WIN, GROUP * WIN), F32),
            pltpu.VMEM((GROUP * WIN, 2 * WIN), F32),
        ],
        compiler_params=pltpu.CompilerParams(vmem_limit_bytes=60 << 20),
        name="tile_step",
    )(offsets, tiles, pupils, intensity, seeds, fwd, inv, lanes, sides)


def row_tables():
    lane = np.arange(128)
    k1 = np.arange(32)
    turn = unit(-(k1[:, None] * lane[None, :]) / ROWS)
    keep = axis_filter(ROWS)[k1[:, None] + 32 * lane[None, :]]
    rows = np.stack([turn.real, turn.imag, keep.real, keep.imag]).astype(np.float32)
    full = dft_np(128, -1)
    mats = np.stack([*split_np(right_block(full)), *split_np(right_block(np.conj(full)))])
    return rows, mats


def row_body(got, rows, mats, out, work, mid):
    lane = lax.broadcasted_iota(jnp.int32, (8, 128), 1)
    ramp = jnp.where(lane < OVL, (lane.astype(F32) + 0.5) / OVL, 1.0)
    rest = jnp.where(lane < OVL, 1.0 - ramp, 0.0)

    @pl.loop(0, 8)
    def _(g):
        at = pl.ds(pl.multiple_of(g * 8, 8), 8)
        for a in range(4):
            items = []
            for p in range(8):
                re = got[p, at, 128 * a : 128 * a + 128]
                im = got[p, at, STRIDE + 128 * a : STRIDE + 128 * a + 128]
                if a == 0:
                    tail = got[(p - 1) % 8, at, 2 * STRIDE :]
                    re = ramp * re + rest * tail
                    im = ramp * im + rest * pltpu.roll(tail, 64, 1)
                items.append((re, im))
            done = fft_list(items, -1)
            for k in range(8):
                re, im = cscale(done[k], unit(-a * k / 32))
                mid[4 * k + a, 0, at, :] = re
                mid[4 * k + a, 1, at, :] = im

        @pl.loop(0, 8)
        def _(k):
            items = [(mid[4 * k + a, 0, at, :], mid[4 * k + a, 1, at, :]) for a in range(4)]
            done = fft_list(items, -1)
            for q in range(4):
                index = k + 8 * q
                tr = rows[0, pl.ds(index, 1), :]
                ti = rows[1, pl.ds(index, 1), :]
                re, im = cmul(*done[q], tr, ti)
                start = pl.ds(pl.multiple_of(index * 64 + g * 8, 8), 8)
                work[start, :128] = re
                work[start, 128:] = im

    @pl.loop(0, 4)
    def _(n):
        at = pl.ds(pl.multiple_of(n * 512, 512), 512)
        full = mm3(split(work[at, :]), (mats[0], mats[1]))
        full = full.reshape(8, 64, 256)
        keep = pl.ds(pl.multiple_of(n * 8, 8), 8)
        kr, ki = rows[2, keep, :][:, None, :], rows[3, keep, :][:, None, :]
        re, im = cmul(full[:, :, :128], full[:, :, 128:], kr, ki)
        both = jnp.concatenate([re, im], axis=2).reshape(512, 256)
        work[at, :] = mm3(split(both), (mats[2], mats[3]))

    @pl.loop(0, 8)
    def _(g):
        at = pl.ds(pl.multiple_of(g * 8, 8), 8)

        @pl.loop(0, 8)
        def _(k):
            items = []
            for q in range(4):
                index = k + 8 * q
                tr = rows[0, pl.ds(index, 1), :]
                ti = rows[1, pl.ds(index, 1), :]
                start = pl.ds(pl.multiple_of(index * 64 + g * 8, 8), 8)
                items.append(cmul(work[start, :128], work[start, 128:], tr, -ti))
            done = fft_list(items, 1)
            for a in range(4):
                mid[4 * k + a, 0, at, :] = done[a][0]
                mid[4 * k + a, 1, at, :] = done[a][1]

        for a in range(4):
            items = [
                cscale((mid[4 * k + a, 0, at, :], mid[4 * k + a, 1, at, :]), unit(a * k / 32))
                for k in range(8)
            ]
            done = fft_list(items, 1)
            for p in range(8):
                mid[4 * p + a, 0, at, :] = done[p][0]
                mid[4 * p + a, 1, at, :] = done[p][1]

    @pl.loop(0, 32)
    def _(a):
        out[a] = jnp.transpose(mid[a].reshape(128, 128))


def row_step(got):
    rows, mats = row_tables()
    return pl.pallas_call(
        row_body,
        out_shape=jax.ShapeDtypeStruct((32, 128, 128), F32),
        in_specs=[vmem()] * 3,
        out_specs=vmem(),
        scratch_shapes=[
            pltpu.VMEM((2048, 256), F32),
            pltpu.VMEM((32, 2, 64, 128), F32),
        ],
        compiler_params=pltpu.CompilerParams(vmem_limit_bytes=40 << 20),
        name="row_step",
    )(got, rows, mats)


def col_tables():
    lane = np.arange(64)
    kc = np.arange(16)
    kr = np.arange(8)
    low = kc[None, :] + 16 * kr[:, None]
    turn = unit(-(low[:, :, None] * lane) / COLS)
    keep = axis_filter(COLS)[low[:, :, None] + 128 * lane]
    rows = np.stack([turn.real, turn.imag, keep.real, keep.imag]).reshape(4, 128, 64)
    rows = np.concatenate([rows, rows], axis=2).astype(np.float32)
    inner = unit(-(np.arange(8)[:, None] * kc[None, :]) / 128)
    full = np.kron(np.eye(2), dft_np(64, -1))
    mats = np.stack([*split_np(right_block(full)), *split_np(right_block(np.conj(full)))])
    return rows, mats, inner


def col_body(got, rows, mats, out, work, mid):
    left = lax.broadcasted_iota(jnp.int32, (8, 128), 1) < 64
    inner = col_tables()[2]

    for half in range(2):
        at = slice(8 * half, 8 * half + 8)
        for r in range(8):
            items = []
            for c in range(16):
                a = got[16 * r + c, 8 * half : 8 * half + 8, :]
                b = got[16 * r + c, 16 + 8 * half : 24 + 8 * half, :]
                re = jnp.where(left, a, pltpu.roll(b, 64, 1))
                im = jnp.where(left, pltpu.roll(a, 64, 1), b)
                items.append((re, im))
            done = fft_list(items, -1)
            for k in range(16):
                re, im = cscale(done[k], inner[r, k])
                mid[16 * r + k, 0, at, :] = re
                mid[16 * r + k, 1, at, :] = im

    @pl.loop(0, 16)
    def _(k):
        for half in range(2):
            at = slice(8 * half, 8 * half + 8)
            items = [(mid[16 * r + k, 0, at, :], mid[16 * r + k, 1, at, :]) for r in range(8)]
            done = fft_list(items, -1)
            for q in range(8):
                index = 16 * q + k
                tr = rows[0, pl.ds(index, 1), :]
                ti = rows[1, pl.ds(index, 1), :]
                re, im = cmul(*done[q], tr, ti)
                work[index, at, :128] = re
                work[index, at, 128:] = im

    @pl.loop(0, 4)
    def _(n):
        keep = pl.ds(pl.multiple_of(n * 32, 32), 32)
        full = mm3(split(work[keep].reshape(512, 256)), (mats[0], mats[1]))
        full = full.reshape(32, 16, 256)
        kr, ki = rows[2, keep, :][:, None, :], rows[3, keep, :][:, None, :]
        re, im = cmul(full[:, :, :128], full[:, :, 128:], kr, ki)
        both = jnp.concatenate([re, im], axis=2).reshape(512, 256)
        work[keep] = mm3(split(both), (mats[2], mats[3])).reshape(32, 16, 256)

    @pl.loop(0, 16)
    def _(k):
        for half in range(2):
            at = slice(8 * half, 8 * half + 8)
            items = []
            for q in range(8):
                index = 16 * q + k
                tr = rows[0, pl.ds(index, 1), :]
                ti = rows[1, pl.ds(index, 1), :]
                items.append(cmul(work[index, at, :128], work[index, at, 128:], tr, -ti))
            done = fft_list(items, 1)
            for r in range(8):
                mid[16 * r + k, 0, at, :] = done[r][0]
                mid[16 * r + k, 1, at, :] = done[r][1]

    for half in range(2):
        at = slice(8 * half, 8 * half + 8)
        for r in range(8):
            items = [
                cscale((mid[16 * r + k, 0, at, :], mid[16 * r + k, 1, at, :]), np.conj(inner[r, k]))
                for k in range(16)
            ]
            done = fft_list(items, 1)
            for c in range(16):
                mid[16 * r + c, 0, at, :] = done[c][0]
                mid[16 * r + c, 1, at, :] = done[c][1]

    @pl.loop(0, 16)
    def _(c):
        for part in range(2):
            for half in range(2):
                at = slice(8 * half, 8 * half + 8)
                for pair in range(4):
                    a = mid[32 * pair + c, part, at, :]
                    b = mid[32 * pair + 16 + c, part, at, :]
                    lanes = slice(128 * pair, 128 * pair + 128)
                    top = pl.ds(pl.multiple_of(c * 32 + 8 * half, 8), 8)
                    low = pl.ds(pl.multiple_of(c * 32 + 16 + 8 * half, 8), 8)
                    out[part, top, lanes] = jnp.where(left, a, pltpu.roll(b, 64, 1))
                    out[part, low, lanes] = jnp.where(left, pltpu.roll(a, 64, 1), b)


def col_step(got):
    rows, mats, _ = col_tables()
    return pl.pallas_call(
        col_body,
        out_shape=jax.ShapeDtypeStruct((2, 512, 512), F32),
        in_specs=[vmem()] * 3,
        out_specs=vmem(),
        scratch_shapes=[
            pltpu.VMEM((128, 16, 256), F32),
            pltpu.VMEM((128, 2, 16, 128), F32),
        ],
        compiler_params=pltpu.CompilerParams(vmem_limit_bytes=40 << 20),
        name="col_step",
    )(got, rows, mats)


def local(tiles, pupils, intensity, offsets):
    refined = tile_step(tiles, pupils, intensity, offsets[0, 0])
    pairs = [(source, (source + 1) % 16) for source in range(16)]
    behind = lax.ppermute(refined[STRIDE:], "col", pairs)
    ramp = ((jnp.arange(OVL, dtype=F32) + 0.5) / OVL)[:, None]
    front = ramp * refined[:OVL] + (1.0 - ramp) * behind
    field = lax.dynamic_update_slice(refined[:STRIDE], front, (0, 0))
    field = field.reshape(8, 64, 2 * TILE)
    field = lax.all_to_all(field, "row", split_axis=0, concat_axis=0, tiled=True)
    field = row_step(field).reshape(128, 32, 128)
    field = lax.all_to_all(field, ("row", "col"), split_axis=0, concat_axis=0, tiled=True)
    field = col_step(field)
    return lax.all_to_all(field, "col", split_axis=1, concat_axis=1, tiled=True)


def solution(mesh):
    placed = (
        P(None, "row", "col"),
        P(None, "row", "col"),
        P(None, "row", "col"),
        P("row", "col", None, None),
    )
    return jax.shard_map(
        local, mesh=mesh, in_specs=placed, out_specs=P(None, "row", "col"), check_vma=False
    )
```

time: 987 us -> 168 us (0.17); the launches traced: 972 us -> 168 us
  matrix products: 333 us -> 0 us
  local copies, waits for them, and re-layouts: 155 us -> 4.48 us
  waiting for transfers between devices: 142 us -> 3.66 us
  blocking collectives: 217 us -> 105 us
  loops' own time: 59.6 us -> 0 us
  Pallas kernels: 0 us -> 52 us
  other arithmetic: 32.7 us -> 0.11 us
  starting transfers between devices: 31 us -> 2.67 us
    dot_general x64 -> x0, matrix products: 333 us -> none  [product(): return jnp.einsum(form, left, right, precision=lax.Precision.HIGHEST)]
    all_to_all x5 -> x0, waiting for transfers between devices: 128 us -> none  [the longest x3 80.9 us: column_swap(): lax.all_to_all(values, 'col', split_axis=2, concat_axis=2, tiled=True)]
    all_to_all x7 -> x3, blocking collectives: 217 us -> 105 us  [the longest x1 40.8 us: local(): lax.all_to_all(field, ('row', 'col'), split_axis=0, concat_axis=0, tiled=...]
    another operation x2 -> x0, loops' own time: 59.6 us -> none  [the longest x1 59.4 us: local(): total = lax.fori_loop(0, led_count, place, jnp.zeros_like(spectrum))]
    pallas_call x0 -> x3, Pallas kernels: none -> 52 us  [the longest x1 33.9 us: tile_step(): pl.pallas_call(tile_body, out_shape=jax.ShapeDtypeStruct((TILE, 2 * TILE)...]
    gather x48 -> x0, local copies, waits for them, and re-layouts: 47.6 us -> none
    dynamic_update_slice x16 -> x0, local copies, waits for them, and re-layouts: 39 us -> none  [place(): return lax.dynamic_update_slice(total, current + updates[led], corner)]
    all_to_all x5 -> x0, starting transfers between devices: 27.4 us -> none  [the longest x3 19.6 us: column_swap(): lax.all_to_all(values, 'col', split_axis=2, concat_axis=2, tiled=True)]
  transfers between devices with their start and end apart: 7 -> 1, of which waited for: 7 -> 1; matrix products, arithmetic and copies ran while one was open for 0% -> 0% of each run, Pallas kernels for 0% -> 0%
where the time goes in v1:
time: 168 us
  blocking collectives  105 us (62%)
  Pallas kernels  52 us (31%)
  local copies, waits for them, and re-layouts  4.48 us (3%)
  waiting for transfers between devices  3.66 us (2%)
  starting transfers between devices  2.67 us (2%)
    all_to_all x1, blocking collectives, local(): lax.all_to_all(field, ('row', 'col'), split_axis=0, concat_axis=0, tiled=...  40.8 us
    pallas_call x1, Pallas kernels, tile_step(): pl.pallas_call(tile_body, out_shape=jax.ShapeDtypeStruct((TILE, 2 * TILE)...  33.9 us
    all_to_all x1, blocking collectives, local(): lax.all_to_all(field, 'row', split_axis=0, concat_axis=0, tiled=True)  33.7 us
    all_to_all x1, blocking collectives, local(): return lax.all_to_all(field, 'col', split_axis=1, concat_axis=1, tiled=True)  30.4 us
    pallas_call x1, Pallas kernels, row_step(): pl.pallas_call(row_body, out_shape=jax.ShapeDtypeStruct((32, 128, 128), F...  10.1 us
    pallas_call x1, Pallas kernels, col_step(): pl.pallas_call(col_body, out_shape=jax.ShapeDtypeStruct((2, 512, 512), F3...  7.99 us
    ppermute x1, waiting for transfers between devices, local(): behind = lax.ppermute(refined[STRIDE:], 'col', pairs)  3.66 us
  transfers between devices with their start and end apart: 1, of which 1 were waited for; matrix products, arithmetic and copies ran while one was open for 0% of the time, Pallas kernels for 0%

profile of v1, /device:TPU:1, one launch (start us, length us, event | category | flops | bytes accessed | tf_op | source)
XLA Modules:
  0.0 167.8 jit_solution(15951857174382332968)
XLA Ops:
  0.0 33.9 %tile_step.1 = f32[576,1152]{1,0:T(8,128)} custom-call(s32[2,16]{1,0:T(2,128)} %bitcast.5, f32[2,576,576]{2,1,0:T(8,128)} %tiles.1, f32[2,128,128]{2,1,0:T(8,128)} %pupils.1, f32[16,128,128]{2,1,0:T(8,128)} %intensity.1, f32[4,24,640]{2,1,0:T(8,128)} %constant.27.clone.seeds, bf16[2,6,192,192]{3,2,1,0:T(8,128)(2,1)} %constant.28.clone.fwd, ...), custom_call_target="tpu_custom_call" | custom-call | tf_op jit(solution)/shard_map/tile_step/pallas_call | solution.py:358
  33.9 0.0 copy-start.4
  33.9 1.1 slice.14
  35.0 0.0 slice-start
  35.0 2.7 %collective-permute-start = (f32[64,1152]{1,0:T(8,128)S(1)}, f32[64,1152]{1,0:T(8,128)S(1)}, u32[]{:S(2)}, u32[]{:S(2)}) collective-permute-start(f32[64,1152]{1,0:T(8,128)S(1)} %slice.14), channel_id=1, source_target_pairs={{0,1},{1,2},{2,3},{3,4},{4,5},{5,6},{6,7},{7,8},{8,9},{9,10},{10,1... | collective-permute-start | bytes 884744 | tf_op jit(solution)/shard_map/ppermute | solution.py:613
  37.7 3.7 %collective-permute-done = f32[64,1152]{1,0:T(8,128)S(1)} collective-permute-done((f32[64,1152]{1,0:T(8,128)S(1)}, f32[64,1152]{1,0:T(8,128)S(1)}, u32[]{:S(2)}, u32[]{:S(2)}) %collective-permute-start) | collective-permute-done | bytes 294944 | tf_op jit(solution)/shard_map/ppermute | solution.py:613
  41.3 0.0 copy-done.4
  41.3 0.0 slice-done
  41.3 0.1 fusion.1
  41.5 0.0 copy-start.1
  41.5 0.0 copy-start.3
  41.5 33.7 %all_to_all.15.got = f32[8,64,1152]{2,1,0:T(8,128)S(1)} all-to-all(f32[8,64,1152]{2,1,0:T(8,128)S(1)} %bitcast.4), channel_id=1, replica_groups=mesh['row'=8,'col'=16] {'row'}, dimensions={0} | all-to-all | bytes 4718592 | tf_op jit(solution)/shard_map/all_to_all | solution.py:618
  75.2 0.0 copy-done.1
  75.2 0.0 copy-done.3
  75.2 10.1 %row_step.1 = f32[32,128,128]{2,1,0:T(8,128)S(1)} custom-call(f32[8,64,1152]{2,1,0:T(8,128)S(1)} %all_to_all.15.got, f32[4,32,128]{2,1,0:T(8,128)S(1)} %copy-done.3, bf16[4,256,256]{2,1,0:T(8,128)(2,1)S(1)} %copy-done.1), custom_call_target="tpu_custom_call" | custom-call | tf_op jit(solution)/shard_map/row_step/pallas_call | solution.py:479
  85.3 0.0 copy-start
  85.3 0.0 copy-start.2
  85.3 40.8 %all_to_all.16.got = f32[128,32,128]{2,1,0:T(8,128)S(1)} all-to-all(f32[128,32,128]{2,1,0:T(8,128)S(1)} %bitcast.3), channel_id=1, replica_groups=mesh['row'=8,'col'=16] {'row','col'}, dimensions={0} | all-to-all | bytes 4194304 | tf_op jit(solution)/shard_map/all_to_all | solution.py:620
  126.1 0.0 copy-done
  126.1 0.0 copy-done.2
  126.1 8.0 %col_step.1 = f32[2,512,512]{2,1,0:T(8,128)S(1)} custom-call(f32[128,32,128]{2,1,0:T(8,128)S(1)} %all_to_all.16.got, f32[4,128,128]{2,1,0:T(8,128)S(1)} %copy-done.2, bf16[4,256,256]{2,1,0:T(8,128)(2,1)S(1)} %copy-done), custom_call_target="tpu_custom_call" | custom-call | tf_op jit(solution)/shard_map/col_step/pallas_call | solution.py:596
  134.1 1.6 copy.14
  135.7 30.4 %all_to_all.17 = f32[2,512,512]{2,0,1:T(2,128)S(1)} all-to-all(f32[2,512,512]{2,0,1:T(2,128)S(1)} %copy.14), channel_id=1, replica_groups=mesh['row'=8,'col'=16] {'col'}, dimensions={1} | all-to-all | bytes 4194304 | tf_op jit(solution)/shard_map/all_to_all | solution.py:622
  166.1 1.7 %copy.15 = f32[2,512,512]{2,1,0:T(8,128)} copy(f32[2,512,512]{2,0,1:T(2,128)S(1)} %all_to_all.17) | data formatting | bytes 4194304 | tf_op jit(solution)/shard_map/all_to_all | solution.py:622
  (1 shorter events, 0.0 us)
Async XLA Ops:
  33.9 7.5 %copy-start.4 = (f32[576,1152]{1,0:T(8,128)S(1)}, f32[576,1152]{1,0:T(8,128)}, u32[]{:S(2)}) copy-start(f32[576,1152]{1,0:T(8,128)} %tile_step.1) | copy-start | bytes 7962628
  35.0 6.4 %slice-start = ((f32[576,1152]{1,0:T(8,128)}), f32[512,1152]{1,0:T(8,128)S(1)}, s32[]{:S(2)}) async-start(f32[576,1152]{1,0:T(8,128)} %tile_step.1), calls=%async_computation.3 | async-start | bytes 4718592 | tf_op jit(solution)/shard_map/slice | solution.py:616
  35.0 6.3 %collective-permute-start = (f32[64,1152]{1,0:T(8,128)S(1)}, f32[64,1152]{1,0:T(8,128)S(1)}, u32[]{:S(2)}, u32[]{:S(2)}) collective-permute-start(f32[64,1152]{1,0:T(8,128)S(1)} %slice.14), channel_id=1, source_target_pairs={{0,1},{1,2},{2,3},{3,4},{4,5},{5,6},{6,7},{7,8},{8,9},{9,10},{10,1... | collective-permute-start | bytes 884744 | tf_op jit(solution)/shard_map/ppermute | solution.py:613
  41.5 33.7 %copy-start.1 = (bf16[4,256,256]{2,1,0:T(8,128)(2,1)S(1)}, bf16[4,256,256]{2,1,0:T(8,128)(2,1)}, u32[]{:S(2)}) copy-start(bf16[4,256,256]{2,1,0:T(8,128)(2,1)} %constant.33.clone.mats) | copy-start | bytes 1572868
  41.5 33.7 %copy-start.3 = (f32[4,32,128]{2,1,0:T(8,128)S(1)}, f32[4,32,128]{2,1,0:T(8,128)}, u32[]{:S(2)}) copy-start(f32[4,32,128]{2,1,0:T(8,128)} %constant.32.clone.rows) | copy-start | bytes 196612
  85.3 40.8 %copy-start = (bf16[4,256,256]{2,1,0:T(8,128)(2,1)S(1)}, bf16[4,256,256]{2,1,0:T(8,128)(2,1)}, u32[]{:S(2)}) copy-start(bf16[4,256,256]{2,1,0:T(8,128)(2,1)} %constant.35.clone.mats) | copy-start | bytes 1572868
  85.3 40.8 %copy-start.2 = (f32[4,128,128]{2,1,0:T(8,128)S(1)}, f32[4,128,128]{2,1,0:T(8,128)}, u32[]{:S(2)}) copy-start(f32[4,128,128]{2,1,0:T(8,128)} %constant.34.clone.rows) | copy-start | bytes 786436

commit v2 on v1

--- a/solution.py
+++ b/solution.py
@@ -393,103 +393,6 @@
     return rows, mats
 
 
-def row_body(got, rows, mats, out, work, mid):
-    lane = lax.broadcasted_iota(jnp.int32, (8, 128), 1)
-    ramp = jnp.where(lane < OVL, (lane.astype(F32) + 0.5) / OVL, 1.0)
-    rest = jnp.where(lane < OVL, 1.0 - ramp, 0.0)
-
-    @pl.loop(0, 8)
-    def _(g):
-        at = pl.ds(pl.multiple_of(g * 8, 8), 8)
-        for a in range(4):
-            items = []
-            for p in range(8):
-                re = got[p, at, 128 * a : 128 * a + 128]
-                im = got[p, at, STRIDE + 128 * a : STRIDE + 128 * a + 128]
-                if a == 0:
-                    tail = got[(p - 1) % 8, at, 2 * STRIDE :]
-                    re = ramp * re + rest * tail
-                    im = ramp * im + rest * pltpu.roll(tail, 64, 1)
-                items.append((re, im))
-            done = fft_list(items, -1)
-            for k in range(8):
-                re, im = cscale(done[k], unit(-a * k / 32))
-                mid[4 * k + a, 0, at, :] = re
-                mid[4 * k + a, 1, at, :] = im
-
-        @pl.loop(0, 8)
-        def _(k):
-            items = [(mid[4 * k + a, 0, at, :], mid[4 * k + a, 1, at, :]) for a in range(4)]
-            done = fft_list(items, -1)
-            for q in range(4):
-                index = k + 8 * q
-                tr = rows[0, pl.ds(index, 1), :]
-                ti = rows[1, pl.ds(index, 1), :]
-                re, im = cmul(*done[q], tr, ti)
-                start = pl.ds(pl.multiple_of(index * 64 + g * 8, 8), 8)
-                work[start, :128] = re
-                work[start, 128:] = im
-
-    @pl.loop(0, 4)
-    def _(n):
-        at = pl.ds(pl.multiple_of(n * 512, 512), 512)
-        full = mm3(split(work[at, :]), (mats[0], mats[1]))
-        full = full.reshape(8, 64, 256)
-        keep = pl.ds(pl.multiple_of(n * 8, 8), 8)
-        kr, ki = rows[2, keep, :][:, None, :], rows[3, keep, :][:, None, :]
-        re, im = cmul(full[:, :, :128], full[:, :, 128:], kr, ki)
-        both = jnp.concatenate([re, im], axis=2).reshape(512, 256)
-        work[at, :] = mm3(split(both), (mats[2], mats[3]))
-
-    @pl.loop(0, 8)
-    def _(g):
-        at = pl.ds(pl.multiple_of(g * 8, 8), 8)
-
-        @pl.loop(0, 8)
-        def _(k):
-            items = []
-            for q in range(4):
-                index = k + 8 * q
-                tr = rows[0, pl.ds(index, 1), :]
-                ti = rows[1, pl.ds(index, 1), :]
-                start = pl.ds(pl.multiple_of(index * 64 + g * 8, 8), 8)
-                items.append(cmul(work[start, :128], work[start, 128:], tr, -ti))
-            done = fft_list(items, 1)
-            for a in range(4):
-                mid[4 * k + a, 0, at, :] = done[a][0]
-                mid[4 * k + a, 1, at, :] = done[a][1]
-
-        for a in range(4):
-            items = [
-                cscale((mid[4 * k + a, 0, at, :], mid[4 * k + a, 1, at, :]), unit(a * k / 32))
-                for k in range(8)
-            ]
-            done = fft_list(items, 1)
-            for p in range(8):
-                mid[4 * p + a, 0, at, :] = done[p][0]
-                mid[4 * p + a, 1, at, :] = done[p][1]
-
-    @pl.loop(0, 32)
-    def _(a):
-        out[a] = jnp.transpose(mid[a].reshape(128, 128))
-
-
-def row_step(got):
-    rows, mats = row_tables()
-    return pl.pallas_call(
-        row_body,
-        out_shape=jax.ShapeDtypeStruct((32, 128, 128), F32),
-        in_specs=[vmem()] * 3,
-        out_specs=vmem(),
-        scratch_shapes=[
-            pltpu.VMEM((2048, 256), F32),
-            pltpu.VMEM((32, 2, 64, 128), F32),
-        ],
-        compiler_params=pltpu.CompilerParams(vmem_limit_bytes=40 << 20),
-        name="row_step",
-    )(got, rows, mats)
-
-
 def col_tables():
     lane = np.arange(64)
     kc = np.arange(16)
@@ -505,121 +408,354 @@
     return rows, mats, inner
 
 
-def col_body(got, rows, mats, out, work, mid):
-    left = lax.broadcasted_iota(jnp.int32, (8, 128), 1) < 64
+MESH = pl.DeviceIdType.MESH
+FAR_ROWS = ((1, 2), (1, 1), (1, 3), (0, 2), (1, 0), (0, 1), (0, 3))
+FAR_COLS = sorted(
+    ((y, x, k) for y in range(4) for x in range(2) for k in range(2) if y or x or k),
+    key=lambda step: -(min(step[0], 4 - step[0]) + step[1]),
+)
+QUARTER = 16
+
+
+def settle(ref, sem):
+    pltpu.make_async_copy(ref, ref, sem).wait()
+
+
+def field_body(
+    refined, r_rows, r_mats, c_rows, c_mats, out,
+    halo, front, got, work, mid, give, have, send,
+    halo_sem, send_sem, recv_row, own_row, recv_all, own_all, recv_col, own_sem,
+):
+    row, col = lax.axis_index("row"), lax.axis_index("col")
+    xh, z = row // 4, lax.rem(row, 4)
+    y, xl, core = col // 4, lax.rem(col // 2, 2), lax.rem(col, 2)
+    rows_at = [lax.rem(row + step, 8) for step in range(8)]
+    cols_at = [lax.rem(col + step, 16) for step in range(16)]
+
+    barrier = pltpu.get_barrier_semaphore()
+    for i in range(8):
+        for j in range(16):
+            if i or j:
+                pl.semaphore_signal(
+                    barrier, inc=1, device_id=(rows_at[i], cols_at[j]), device_id_type=MESH
+                )
+    pl.semaphore_wait(barrier, 127)
+
+    edge = pltpu.make_async_remote_copy(
+        refined.at[STRIDE:], halo, halo_sem.at[0], halo_sem.at[1],
+        device_id=(row, cols_at[1]), device_id_type=MESH,
+    )
+    edge.start()
+
+    chunks = [lax.rem(xh + i, 2) * 4 + lax.rem(z + j, 4) for i, j in FAR_ROWS]
+
+    def give_row(target, quarter, source):
+        pltpu.make_async_remote_copy(
+            source, got.at[row, quarter * QUARTER : (quarter + 1) * QUARTER],
+            send_sem.at[0], recv_row.at[quarter], device_id=(target, col), device_id_type=MESH,
+        ).start()
+
+    def plain(target, quarter):
+        start = pl.multiple_of(target * 64 + quarter * QUARTER, QUARTER)
+        return refined.at[pl.ds(start, QUARTER)]
+
+    def blended(quarter):
+        return front.at[quarter * QUARTER : (quarter + 1) * QUARTER]
+
+    for target in chunks:
+        @pl.when(target != 0)
+        def _():
+            give_row(target, 0, plain(target, 0))
+
+    edge.wait()
+    place = lax.broadcasted_iota(jnp.int32, (OVL, 2 * TILE), 0).astype(F32)
+    ramp = (place + 0.5) / OVL
+    front[...] = ramp * refined[:OVL] + (1.0 - ramp) * halo[...]
+
+    for target in chunks:
+        @pl.when(target == 0)
+        def _():
+            give_row(target, 0, blended(0))
+
+    for quarter in range(1, 4):
+        for target in chunks:
+            @pl.when(target != 0)
+            def _():
+                give_row(target, quarter, plain(target, quarter))
+
+            @pl.when(target == 0)
+            def _():
+                give_row(target, quarter, blended(quarter))
+
+    @pl.when(row == 0)
+    def _():
+        pltpu.make_async_copy(front, got.at[0], own_row).start()
+
+    @pl.when(row != 0)
+    def _():
+        start = pl.multiple_of(row * 64, 64)
+        pltpu.make_async_copy(refined.at[pl.ds(start, 64)], got.at[row], own_row).start()
+
+    settle(front, own_row)
+
+    lane = lax.broadcasted_iota(jnp.int32, (8, 128), 1)
+    slope = jnp.where(lane < OVL, (lane.astype(F32) + 0.5) / OVL, 1.0)
+    rest = jnp.where(lane < OVL, 1.0 - slope, 0.0)
+
+    @pl.loop(0, 4)
+    def _(quarter):
+        columns = pl.ds(pl.multiple_of(quarter * QUARTER, QUARTER), QUARTER)
+        settle(got.at[:7, columns], recv_row.at[quarter])
+
+        @pl.loop(0, 2)
+        def _(half):
+            at = pl.ds(pl.multiple_of(quarter * QUARTER + half * 8, 8), 8)
+            for a in range(4):
+                items = []
+                for p in range(8):
+                    re = got[p, at, 128 * a : 128 * a + 128]
+                    im = got[p, at, STRIDE + 128 * a : STRIDE + 128 * a + 128]
+                    if a == 0:
+                        tail = got[(p - 1) % 8, at, 2 * STRIDE :]
+                        re = slope * re + rest * tail
+                        im = slope * im + rest * pltpu.roll(tail, 64, 1)
+                    items.append((re, im))
+                done = fft_list(items, -1)
+                for k in range(8):
+                    re, im = cscale(done[k], unit(-a * k / 32))
+                    mid[4 * k + a, 0, at, :] = re
+                    mid[4 * k + a, 1, at, :] = im
+
+            @pl.loop(0, 8)
+            def _(k):
+                items = [(mid[4 * k + a, 0, at, :], mid[4 * k + a, 1, at, :]) for a in range(4)]
+                done = fft_list(items, -1)
+                for q in range(4):
+                    index = k + 8 * q
+                    tr = r_rows[0, pl.ds(index, 1), :]
+                    ti = r_rows[1, pl.ds(index, 1), :]
+                    re, im = cmul(*done[q], tr, ti)
+                    start = pl.ds(pl.multiple_of(index * QUARTER + half * 8, 8), 8)
+                    work[start, :128] = re
+                    work[start, 128:] = im
+
+        full = mm3(split(work[:512]), (r_mats[0], r_mats[1]))
+        full = full.reshape(32, QUARTER, 256)
+        kr, ki = r_rows[2][:, None, :], r_rows[3][:, None, :]
+        re, im = cmul(full[:, :, :128], full[:, :, 128:], kr, ki)
+        both = jnp.concatenate([re, im], axis=2).reshape(512, 256)
+        work[:512] = mm3(split(both), (r_mats[2], r_mats[3]))
+
+        @pl.loop(0, 2)
+        def _(half):
+            at = pl.ds(pl.multiple_of(quarter * QUARTER + half * 8, 8), 8)
+
+            @pl.loop(0, 8)
+            def _(k):
+                items = []
+                for q in range(4):
+                    index = k + 8 * q
+                    tr = r_rows[0, pl.ds(index, 1), :]
+                    ti = r_rows[1, pl.ds(index, 1), :]
+                    start = pl.ds(pl.multiple_of(index * QUARTER + half * 8, 8), 8)
+                    items.append(cmul(work[start, :128], work[start, 128:], tr, -ti))
+                done = fft_list(items, 1)
+                for a in range(4):
+                    mid[4 * k + a, 0, at, :] = done[a][0]
+                    mid[4 * k + a, 1, at, :] = done[a][1]
+
+            for a in range(4):
+                items = [
+                    cscale((mid[4 * k + a, 0, at, :], mid[4 * k + a, 1, at, :]), unit(a * k / 32))
+                    for k in range(8)
+                ]
+                done = fft_list(items, 1)
+                for p in range(8):
+                    mid[4 * p + a, 0, at, :] = done[p][0]
+                    mid[4 * p + a, 1, at, :] = done[p][1]
+
+    me = row * 16 + col
+
+    def peers(step):
+        tr = lax.rem(xh + 1 + step // 16, 2) * 4 + lax.rem(z + 2 + (step // 4) % 4, 4)
+        ty = lax.rem(y + 2 + step % 4, 4)
+        ends = []
+        for i in range(2):
+            for j in range(2):
+                ends.append((tr, ty * 4 + lax.rem(xl + i, 2) * 2 + lax.rem(core + j, 2)))
+        return tr * 4 + ty, ends
+
+    own_step = 26
+
+    def give_all(step, ends, part):
+        lines = slice(part * 16, part * 16 + 16)
+        for index, (tr, tc) in enumerate(ends):
+            def go(tr=tr, tc=tc):
+                pltpu.make_async_remote_copy(
+                    give.at[tr * 16 + tc, lines], have.at[me, lines],
+                    send_sem.at[1], recv_all.at[part], device_id=(tr, tc), device_id_type=MESH,
+                ).start()
+
+            if index:
+                go()
+            else:
+                pl.when(step != own_step)(go)
+
+    @pl.loop(0, 32)
+    def _(step):
+        block, ends = peers(step)
+        flat = jnp.transpose(mid[block].reshape(128, 128))
+        for i in range(4):
+            give[block * 4 + i] = flat[32 * i : 32 * i + 32]
+        give_all(step, ends, 0)
+
+    own = pltpu.make_async_copy(give.at[me], have.at[me], own_all)
+    own.start()
+
+    @pl.loop(0, 32)
+    def _(step):
+        give_all(step, peers(step)[1], 1)
+
+    own.wait()
+
+    left = lane < 64
     inner = col_tables()[2]
 
-    for half in range(2):
-        at = slice(8 * half, 8 * half + 8)
+    @pl.loop(0, 2)
+    def _(part):
+        lines = pl.ds(pl.multiple_of(part * 16, 16), 16)
+        top = pl.ds(pl.multiple_of(part * 16, 8), 8)
+        low = pl.ds(pl.multiple_of(part * 16 + 8, 8), 8)
+        settle(have.at[:127, lines], recv_all.at[part])
+
         for r in range(8):
             items = []
             for c in range(16):
-                a = got[16 * r + c, 8 * half : 8 * half + 8, :]
-                b = got[16 * r + c, 16 + 8 * half : 24 + 8 * half, :]
+                a = have[16 * r + c, top, :]
+                b = have[16 * r + c, low, :]
                 re = jnp.where(left, a, pltpu.roll(b, 64, 1))
                 im = jnp.where(left, pltpu.roll(a, 64, 1), b)
                 items.append((re, im))
             done = fft_list(items, -1)
             for k in range(16):
+                flat = 8 * (16 * r + k)
                 re, im = cscale(done[k], inner[r, k])
-                mid[16 * r + k, 0, at, :] = re
-                mid[16 * r + k, 1, at, :] = im
-
-    @pl.loop(0, 16)
-    def _(k):
-        for half in range(2):
-            at = slice(8 * half, 8 * half + 8)
-            items = [(mid[16 * r + k, 0, at, :], mid[16 * r + k, 1, at, :]) for r in range(8)]
+                work[flat : flat + 8, :128] = re
+                work[flat : flat + 8, 128:] = im
+
+        @pl.loop(0, 16)
+        def _(k):
+            places = [pl.ds(pl.multiple_of(8 * (16 * r + k), 8), 8) for r in range(8)]
+            items = [(work[at, :128], work[at, 128:]) for at in places]
             done = fft_list(items, -1)
             for q in range(8):
-                index = 16 * q + k
-                tr = rows[0, pl.ds(index, 1), :]
-                ti = rows[1, pl.ds(index, 1), :]
+                tr = c_rows[0, pl.ds(16 * q + k, 1), :]
+                ti = c_rows[1, pl.ds(16 * q + k, 1), :]
                 re, im = cmul(*done[q], tr, ti)
-                work[index, at, :128] = re
-                work[index, at, 128:] = im
-
-    @pl.loop(0, 4)
-    def _(n):
-        keep = pl.ds(pl.multiple_of(n * 32, 32), 32)
-        full = mm3(split(work[keep].reshape(512, 256)), (mats[0], mats[1]))
-        full = full.reshape(32, 16, 256)
-        kr, ki = rows[2, keep, :][:, None, :], rows[3, keep, :][:, None, :]
-        re, im = cmul(full[:, :, :128], full[:, :, 128:], kr, ki)
-        both = jnp.concatenate([re, im], axis=2).reshape(512, 256)
-        work[keep] = mm3(split(both), (mats[2], mats[3])).reshape(32, 16, 256)
-
-    @pl.loop(0, 16)
-    def _(k):
-        for half in range(2):
-            at = slice(8 * half, 8 * half + 8)
+                work[places[q], :128] = re
+                work[places[q], 128:] = im
+
+        @pl.loop(0, 2)
+        def _(n):
+            at = pl.ds(pl.multiple_of(n * 512, 512), 512)
+            keep = pl.ds(pl.multiple_of(n * 64, 64), 64)
+            full = mm3(split(work[at, :]), (c_mats[0], c_mats[1]))
+            full = full.reshape(64, 8, 256)
+            kr, ki = c_rows[2, keep, :][:, None, :], c_rows[3, keep, :][:, None, :]
+            re, im = cmul(full[:, :, :128], full[:, :, 128:], kr, ki)
+            both = jnp.concatenate([re, im], axis=2).reshape(512, 256)
+            work[at, :] = mm3(split(both), (c_mats[2], c_mats[3]))
+
+        @pl.loop(0, 16)
+        def _(k):
+            places = [pl.ds(pl.multiple_of(8 * (16 * r + k), 8), 8) for r in range(8)]
             items = []
             for q in range(8):
-                index = 16 * q + k
-                tr = rows[0, pl.ds(index, 1), :]
-                ti = rows[1, pl.ds(index, 1), :]
-                items.append(cmul(work[index, at, :128], work[index, at, 128:], tr, -ti))
+                tr = c_rows[0, pl.ds(16 * q + k, 1), :]
+                ti = c_rows[1, pl.ds(16 * q + k, 1), :]
+                items.append(cmul(work[places[q], :128], work[places[q], 128:], tr, -ti))
             done = fft_list(items, 1)
             for r in range(8):
-                mid[16 * r + k, 0, at, :] = done[r][0]
-                mid[16 * r + k, 1, at, :] = done[r][1]
-
-    for half in range(2):
-        at = slice(8 * half, 8 * half + 8)
+                work[places[r], :128] = done[r][0]
+                work[places[r], 128:] = done[r][1]
+
         for r in range(8):
-            items = [
-                cscale((mid[16 * r + k, 0, at, :], mid[16 * r + k, 1, at, :]), np.conj(inner[r, k]))
-                for k in range(16)
-            ]
+            items = []
+            for k in range(16):
+                flat = 8 * (16 * r + k)
+                value = (work[flat : flat + 8, :128], work[flat : flat + 8, 128:])
+                items.append(cscale(value, np.conj(inner[r, k])))
             done = fft_list(items, 1)
             for c in range(16):
-                mid[16 * r + c, 0, at, :] = done[c][0]
-                mid[16 * r + c, 1, at, :] = done[c][1]
-
-    @pl.loop(0, 16)
-    def _(c):
-        for part in range(2):
-            for half in range(2):
-                at = slice(8 * half, 8 * half + 8)
+                flat = 8 * (16 * r + c)
+                work[flat : flat + 8, :128] = done[c][0]
+                work[flat : flat + 8, 128:] = done[c][1]
+
+        @pl.loop(0, 16)
+        def _(c):
+            for piece in range(2):
+                lanes = slice(128 * piece, 128 * piece + 128)
                 for pair in range(4):
-                    a = mid[32 * pair + c, part, at, :]
-                    b = mid[32 * pair + 16 + c, part, at, :]
-                    lanes = slice(128 * pair, 128 * pair + 128)
-                    top = pl.ds(pl.multiple_of(c * 32 + 8 * half, 8), 8)
-                    low = pl.ds(pl.multiple_of(c * 32 + 16 + 8 * half, 8), 8)
-                    out[part, top, lanes] = jnp.where(left, a, pltpu.roll(b, 64, 1))
-                    out[part, low, lanes] = jnp.where(left, pltpu.roll(a, 64, 1), b)
-
-
-def col_step(got):
-    rows, mats, _ = col_tables()
+                    first = pl.ds(pl.multiple_of(8 * (32 * pair + c), 8), 8)
+                    second = pl.ds(pl.multiple_of(8 * (32 * pair + 16 + c), 8), 8)
+                    a = work[first, lanes]
+                    b = work[second, lanes]
+                    to = slice(128 * pair, 128 * pair + 128)
+                    send[c, piece, top, to] = jnp.where(left, a, pltpu.roll(b, 64, 1))
+                    send[c, piece, low, to] = jnp.where(left, pltpu.roll(a, 64, 1), b)
+
+        mine = pl.ds(pl.multiple_of(col * 32 + part * 16, 16), 16)
+        for i, j, k in FAR_COLS:
+            tc = lax.rem(y + i, 4) * 4 + lax.rem(xl + j, 2) * 2 + lax.rem(core + k, 2)
+            pltpu.make_async_remote_copy(
+                send.at[tc, :, lines], out.at[:, mine],
+                send_sem.at[2], recv_col.at[part], device_id=(row, tc), device_id_type=MESH,
+            ).start()
+        pltpu.make_async_copy(send.at[col, :, lines], out.at[:, mine], own_sem.at[part]).start()
+
+    for part in range(2):
+        settle(send.at[:15, :, :16], recv_col.at[part])
+        settle(send.at[0, :, :16], own_sem.at[part])
+    settle(got.at[:7], send_sem.at[0])
+    settle(have.at[:127], send_sem.at[1])
+    settle(send.at[:15], send_sem.at[2])
+
+
+def field_step(refined):
+    r_rows, r_mats = row_tables()
+    c_rows, c_mats, _ = col_tables()
     return pl.pallas_call(
-        col_body,
-        out_shape=jax.ShapeDtypeStruct((2, 512, 512), F32),
-        in_specs=[vmem()] * 3,
+        field_body,
+        out_shape=jax.ShapeDtypeStruct((2, STRIDE, STRIDE), F32),
+        in_specs=[vmem()] * 5,
         out_specs=vmem(),
         scratch_shapes=[
-            pltpu.VMEM((128, 16, 256), F32),
-            pltpu.VMEM((128, 2, 16, 128), F32),
+            pltpu.VMEM((OVL, 2 * TILE), F32),
+            pltpu.VMEM((OVL, 2 * TILE), F32),
+            pltpu.VMEM((8, 64, 2 * TILE), F32),
+            pltpu.VMEM((1024, 256), F32),
+            pltpu.VMEM((32, 2, 64, 128), F32),
+            pltpu.VMEM((128, 32, 128), F32),
+            pltpu.VMEM((128, 32, 128), F32),
+            pltpu.VMEM((16, 2, 32, STRIDE), F32),
+            pltpu.SemaphoreType.DMA((2,)),
+            pltpu.SemaphoreType.DMA((3,)),
+            pltpu.SemaphoreType.DMA((4,)),
+            pltpu.SemaphoreType.DMA(()),
+            pltpu.SemaphoreType.DMA((2,)),
+            pltpu.SemaphoreType.DMA(()),
+            pltpu.SemaphoreType.DMA((2,)),
+            pltpu.SemaphoreType.DMA((2,)),
         ],
-        compiler_params=pltpu.CompilerParams(vmem_limit_bytes=40 << 20),
-        name="col_step",
-    )(got, rows, mats)
+        compiler_params=pltpu.CompilerParams(
+            vmem_limit_bytes=60 << 20, collective_id=0, has_side_effects=True
+        ),
+        name="field_step",
+    )(refined, r_rows, r_mats, c_rows, c_mats)
 
 
 def local(tiles, pupils, intensity, offsets):
-    refined = tile_step(tiles, pupils, intensity, offsets[0, 0])
-    pairs = [(source, (source + 1) % 16) for source in range(16)]
-    behind = lax.ppermute(refined[STRIDE:], "col", pairs)
-    ramp = ((jnp.arange(OVL, dtype=F32) + 0.5) / OVL)[:, None]
-    front = ramp * refined[:OVL] + (1.0 - ramp) * behind
-    field = lax.dynamic_update_slice(refined[:STRIDE], front, (0, 0))
-    field = field.reshape(8, 64, 2 * TILE)
-    field = lax.all_to_all(field, "row", split_axis=0, concat_axis=0, tiled=True)
-    field = row_step(field).reshape(128, 32, 128)
-    field = lax.all_to_all(field, ("row", "col"), split_axis=0, concat_axis=0, tiled=True)
-    field = col_step(field)
-    return lax.all_to_all(field, "col", split_axis=1, concat_axis=1, tiled=True)
+    return field_step(tile_step(tiles, pupils, intensity, offsets[0, 0]))
 
 
 def solution(mesh):

time: 168 us -> 139 us (0.83)
  blocking collectives: 105 us -> 0 us
  Pallas kernels: 52 us -> 135 us
  waiting for transfers between devices: 3.66 us -> 0 us
  starting transfers between devices: 2.67 us -> 0 us
    all_to_all x3 -> x0, blocking collectives: 105 us -> none  [the longest x1 40.8 us: local(): lax.all_to_all(field, ('row', 'col'), split_axis=0, concat_axis=0, tiled=...]
    pallas_call x2 -> x1, Pallas kernels: 18.1 us -> 102 us  [field_step(): pl.pallas_call(field_body, out_shape=jax.ShapeDtypeStruct((2, STRIDE, STR...]
    ppermute x1 -> x0, waiting for transfers between devices: 3.66 us -> none  [local(): behind = lax.ppermute(refined[STRIDE:], 'col', pairs)]
    unnamed x10 -> x1, local copies, waits for them, and re-layouts: 0.03 us -> 3.08 us
    ppermute x1 -> x0, starting transfers between devices: 2.67 us -> none  [local(): behind = lax.ppermute(refined[STRIDE:], 'col', pairs)]
    all_to_all x1 -> x0, local copies, waits for them, and re-layouts: 1.7 us -> none  [local(): return lax.all_to_all(field, 'col', split_axis=1, concat_axis=1, tiled=True)]
  transfers between devices with their start and end apart: 1 -> 0, of which waited for: 1 -> 0; matrix products, arithmetic and copies ran while one was open for 0% -> 0% of each run, Pallas kernels for 0% -> 0%
where the time goes in v2:
time: 139 us
  Pallas kernels  135 us (97%)
  local copies, waits for them, and re-layouts  3.08 us (2%)
    pallas_call x1, Pallas kernels, field_step(): pl.pallas_call(field_body, out_shape=jax.ShapeDtypeStruct((2, STRIDE, STR...  102 us
    pallas_call x1, Pallas kernels, tile_step(): pl.pallas_call(tile_body, out_shape=jax.ShapeDtypeStruct((TILE, 2 * TILE)...  33.8 us
    unnamed x1, local copies, waits for them, and re-layouts  3.08 us

profile of v2, /device:TPU:1, one launch (start us, length us, event | category | flops | bytes accessed | tf_op | source)
XLA Modules:
  0.0 138.5 jit_solution(9825688510335668931)
XLA Ops:
  0.0 33.8 %tile_step.1.refined = f32[576,1152]{1,0:T(8,128)} custom-call(s32[2,16]{1,0:T(2,128)} %bitcast.1, f32[2,576,576]{2,1,0:T(8,128)} %tiles.1, f32[2,128,128]{2,1,0:T(8,128)} %pupils.1, f32[16,128,128]{2,1,0:T(8,128)} %intensity.1, f32[4,24,640]{2,1,0:T(8,128)} %constant.18.clone.seeds, bf16[2,6,192,192]{3,2,1,0:T(8,128)(2,1)} %constant.19.clone.fwd, ...), custom_call_target="tpu_custom_call" | custom-call | tf_op jit(solution)/shard_map/tile_step/pallas_call | solution.py:358
  33.8 101.6 %field_step.1 = f32[2,512,512]{2,1,0:T(8,128)} custom-call(f32[576,1152]{1,0:T(8,128)} %tile_step.1.refined, f32[4,32,128]{2,1,0:T(8,128)} %constant.23.clone.r_rows, bf16[4,256,256]{2,1,0:T(8,128)(2,1)} %constant.24.clone.r_mats, f32[4,128,128]{2,1,0:T(8,128)} %constant.25.clone.c_rows, bf16[4,256,256]{2,1,0:T(8,128)(2,1)} %constant.26.clone.c_mats), custom_call_target="tpu_custom_call" | custom-call | tf_op jit(solution)/shard_map/field_step/pallas_call | solution.py:727
  135.4 3.1 %copy.15 = f32[2,512,512]{2,1,0:T(8,128)} copy(f32[2,512,512]{2,1,0:T(8,128)} %field_step.1) | data formatting | bytes 4194304

commit v3 on v2

--- a/solution.py
+++ b/solution.py
@@ -24,6 +24,8 @@
 BF = jnp.bfloat16
 F32 = jnp.float32
 GROUP = 4
+A_LIMIT = 38
+B_LIMIT = 24
 
 
 def split_np(table):
@@ -179,9 +181,20 @@
 
 
 def tile_body(
-    offs, tiles, pupils, intensity, seeds, fwd, inv, lanes, sides, out,
-    base, t_hi, t_lo, l_hi, l_lo, x_hi, x_lo, y, sub, spec, new, v_hi, v_lo, win_a, win_b,
+    offs, tiles_in, pupils_in, intensity_in, seeds_in, fwd_in, inv_in, lanes_in, sides_in, l_hi, l_lo, v_hi, v_lo,
+    base, t_hi, t_lo, x_hi, x_lo, y, sub, spec, new, win_a, win_b,
+    tiles, pupils, intensity, seeds, fwd, inv, lanes, sides, sems,
 ):
+    sources = (seeds_in, tiles_in, fwd_in, pupils_in, intensity_in, lanes_in, sides_in, inv_in)
+    targets = (seeds, tiles, fwd, pupils, intensity, lanes, sides, inv)
+    loads = [
+        pltpu.make_async_copy(source, target, sems.at[index])
+        for index, (source, target) in enumerate(zip(sources, targets))
+    ]
+    for load in loads:
+        load.start()
+    loads[0].wait()
+
     low_r, low_i = seeds[0], seeds[1]
 
     @pl.loop(0, 24)
@@ -208,11 +221,16 @@
         t_lo[pl.ds(start, 96), :PAD] = cl
         t_hi[pl.ds(start, 96), PAD:] = sh
         t_lo[pl.ds(start, 96), PAD:] = sl
+        l_hi[pl.ds(start, 96), :PAD] = ch
+        l_lo[pl.ds(start, 96), :PAD] = cl
+        l_hi[pl.ds(start, 96), PAD:] = sh
+        l_lo[pl.ds(start, 96), PAD:] = sl
         t_hi[pl.ds(start + PAD, 96), :PAD] = -sh
         t_lo[pl.ds(start + PAD, 96), :PAD] = -sl
         t_hi[pl.ds(start + PAD, 96), PAD:] = ch
         t_lo[pl.ds(start + PAD, 96), PAD:] = cl
 
+    loads[1].wait()
     x_hi[...] = jnp.zeros_like(x_hi)
     x_lo[...] = jnp.zeros_like(x_lo)
 
@@ -230,6 +248,8 @@
         both = mm3((x_hi[...], x_lo[...]), (t_hi[:, at], t_lo[:, at]))
         y[2 * n] = both[:, :128]
         y[2 * n + 1] = both[:, 128:]
+
+    loads[2].wait()
 
     @pl.loop(0, RADIX)
     def _(b):
@@ -259,6 +279,8 @@
     for ref in (spec, new):
         for part in range(2):
             ref[part, TILE:, :] = jnp.zeros((8, PAD), F32)
+    for load in loads[3:]:
+        load.wait()
     pr, pi = pupils[0], pupils[1]
     inv_lanes = (lanes[0], lanes[1])
     fwd_lanes = (lanes[2], lanes[3])
@@ -341,13 +363,6 @@
     put(0, STRIDE, 0, STRIDE)
     put(STRIDE, OVL, 2 * STRIDE, 2 * STRIDE + OVL)
 
-    for at, width in ((0, 256), (256, 256), (512, 256), (768, 256), (1024, 128)):
-        right = (v_hi[at : at + width, :], v_lo[at : at + width, :])
-        left = (t_hi[:TILE, :], t_lo[:TILE, :])
-        out[:, at : at + width] = (
-            mm_nt(left[0], right[0]) + (mm_nt(left[1], right[0]) + mm_nt(left[0], right[1]))
-        )
-
 
 def vmem():
     return pl.BlockSpec(memory_space=pltpu.VMEM)
@@ -357,29 +372,42 @@
     seeds, fwd, inv, lanes, sides = tile_tables()
     return pl.pallas_call(
         tile_body,
-        out_shape=jax.ShapeDtypeStruct((TILE, 2 * TILE), F32),
-        in_specs=[pl.BlockSpec(memory_space=pltpu.SMEM)] + [vmem()] * 8,
-        out_specs=vmem(),
+        out_shape=[
+            jax.ShapeDtypeStruct((TILE, 2 * PAD), BF),
+            jax.ShapeDtypeStruct((TILE, 2 * PAD), BF),
+            jax.ShapeDtypeStruct((2 * TILE, 2 * PAD), BF),
+            jax.ShapeDtypeStruct((2 * TILE, 2 * PAD), BF),
+        ],
+        in_specs=[pl.BlockSpec(memory_space=pltpu.SMEM)]
+        + [pl.BlockSpec(memory_space=pltpu.HBM)] * 8,
+        out_specs=[vmem()] * 4,
         scratch_shapes=[
             pltpu.VMEM((2, TILE, PAD), F32),
             pltpu.VMEM((2 * PAD, 2 * PAD), BF),
             pltpu.VMEM((2 * PAD, 2 * PAD), BF),
-            pltpu.VMEM((16, 128), BF),
-            pltpu.VMEM((16, 128), BF),
             pltpu.VMEM((TILE, 2 * PAD), BF),
             pltpu.VMEM((TILE, 2 * PAD), BF),
             pltpu.VMEM((2 * PAD // 128, TILE, 128), F32),
             pltpu.VMEM((RADIX, 2 * SUB, PAD), F32),
             pltpu.VMEM((2, TILE + 8, PAD), F32),
             pltpu.VMEM((2, TILE + 8, PAD), F32),
-            pltpu.VMEM((2 * TILE, 2 * PAD), BF),
-            pltpu.VMEM((2 * TILE, 2 * PAD), BF),
             pltpu.VMEM((2 * WIN, GROUP * WIN), F32),
             pltpu.VMEM((GROUP * WIN, 2 * WIN), F32),
+            *[
+                pltpu.VMEM(value.shape, value.dtype)
+                for value in (tiles, pupils, intensity, seeds, fwd, inv, lanes, sides)
+            ],
+            pltpu.SemaphoreType.DMA((8,)),
         ],
-        compiler_params=pltpu.CompilerParams(vmem_limit_bytes=60 << 20),
+        compiler_params=pltpu.CompilerParams(vmem_limit_bytes=A_LIMIT << 20),
         name="tile_step",
-    )(offsets, tiles, pupils, intensity, seeds, fwd, inv, lanes, sides)
+    )(
+        offsets,
+        *[
+            pltpu.with_memory_space_constraint(jnp.asarray(value), pltpu.HBM)
+            for value in (tiles, pupils, intensity, seeds, fwd, inv, lanes, sides)
+        ],
+    )
 
 
 def row_tables():
@@ -422,8 +450,8 @@
 
 
 def field_body(
-    refined, r_rows, r_mats, c_rows, c_mats, out,
-    halo, front, got, work, mid, give, have, send,
+    l_hi, l_lo, v_hi, v_lo, r_rows, r_mats, c_rows, c_mats, out,
+    refined, halo, front, got, work, mid, give, have, send,
     halo_sem, send_sem, recv_row, own_row, recv_all, own_all, recv_col, own_sem,
 ):
     row, col = lax.axis_index("row"), lax.axis_index("col")
@@ -439,6 +467,27 @@
                 pl.semaphore_signal(
                     barrier, inc=1, device_id=(rows_at[i], cols_at[j]), device_id_type=MESH
                 )
+
+    chunks = [lax.rem(xh + i, 2) * 4 + lax.rem(z + j, 4) for i, j in FAR_ROWS]
+
+    def columns_of(blocks):
+        places = [pl.ds(pl.multiple_of(block * 64, 64), 64) for block in blocks]
+
+        def fill(at):
+            high = jnp.concatenate([l_hi[place, :] for place in places], axis=0)
+            low = jnp.concatenate([l_lo[place, :] for place in places], axis=0)
+            righl_high, righl_low = v_hi[at, :], v_lo[at, :]
+            value = mm_nt(high, righl_high) + (mm_nt(low, righl_high) + mm_nt(high, righl_low))
+            for index, place in enumerate(places):
+                refined[place, at] = value[64 * index : 64 * index + 64]
+
+        @pl.loop(0, 4)
+        def _(n):
+            fill(pl.ds(pl.multiple_of(n * 256, 256), 256))
+
+        fill(slice(1024, 1152))
+
+    columns_of([8, *chunks[:2]])
     pl.semaphore_wait(barrier, 127)
 
     edge = pltpu.make_async_remote_copy(
@@ -447,8 +496,6 @@
     )
     edge.start()
 
-    chunks = [lax.rem(xh + i, 2) * 4 + lax.rem(z + j, 4) for i, j in FAR_ROWS]
-
     def give_row(target, quarter, source):
         pltpu.make_async_remote_copy(
             source, got.at[row, quarter * QUARTER : (quarter + 1) * QUARTER],
@@ -462,10 +509,17 @@
     def blended(quarter):
         return front.at[quarter * QUARTER : (quarter + 1) * QUARTER]
 
-    for target in chunks:
-        @pl.when(target != 0)
-        def _():
-            give_row(target, 0, plain(target, 0))
+    def give_plain(targets):
+        for target in targets:
+            @pl.when(target != 0)
+            def _():
+                give_row(target, 0, plain(target, 0))
+
+    give_plain(chunks[:2])
+    columns_of(chunks[2:5])
+    give_plain(chunks[2:5])
+    columns_of([*chunks[5:], row])
+    give_plain(chunks[5:])
 
     edge.wait()
     place = lax.broadcasted_iota(jnp.int32, (OVL, 2 * TILE), 0).astype(F32)
@@ -721,15 +775,16 @@
     settle(send.at[:15], send_sem.at[2])
 
 
-def field_step(refined):
+def field_step(l_hi, l_lo, v_hi, v_lo):
     r_rows, r_mats = row_tables()
     c_rows, c_mats, _ = col_tables()
     return pl.pallas_call(
         field_body,
         out_shape=jax.ShapeDtypeStruct((2, STRIDE, STRIDE), F32),
-        in_specs=[vmem()] * 5,
+        in_specs=[vmem()] * 8,
         out_specs=vmem(),
         scratch_shapes=[
+            pltpu.VMEM((TILE, 2 * TILE), F32),
             pltpu.VMEM((OVL, 2 * TILE), F32),
             pltpu.VMEM((OVL, 2 * TILE), F32),
             pltpu.VMEM((8, 64, 2 * TILE), F32),
@@ -748,14 +803,14 @@
             pltpu.SemaphoreType.DMA((2,)),
         ],
         compiler_params=pltpu.CompilerParams(
-            vmem_limit_bytes=60 << 20, collective_id=0, has_side_effects=True
+            vmem_limit_bytes=B_LIMIT << 20, collective_id=0, has_side_effects=True
         ),
         name="field_step",
-    )(refined, r_rows, r_mats, c_rows, c_mats)
+    )(l_hi, l_lo, v_hi, v_lo, r_rows, r_mats, c_rows, c_mats)
 
 
 def local(tiles, pupils, intensity, offsets):
-    return field_step(tile_step(tiles, pupils, intensity, offsets[0, 0]))
+    return field_step(*tile_step(tiles, pupils, intensity, offsets[0, 0]))
 
 
 def solution(mesh):

time: 139 us -> 128 us (0.921)
  the two profiles are of different devices: /device:TPU:1 before, /device:TPU:31 now
where the time goes in v3:
time: 128 us
  Pallas kernels  126 us (98%)
  local copies, waits for them, and re-layouts  2.01 us (2%)
    pallas_call x1, Pallas kernels, field_step(): pl.pallas_call(field_body, out_shape=jax.ShapeDtypeStruct((2, STRIDE, STR...  101 us
    pallas_call x1, Pallas kernels, tile_step(): pl.pallas_call(tile_body, out_shape=[jax.ShapeDtypeStruct((TILE, 2 * PAD)...  25.3 us

profile of v3, /device:TPU:31, one launch (start us, length us, event | category | flops | bytes accessed | tf_op | source)
XLA Modules:
  0.0 128.0 jit_solution(10625154774739730518)
XLA Ops:
  0.0 0.0 copy-start.4
  0.0 0.7 copy-done.4
  0.7 0.0 copy-start
  0.7 0.0 copy-start.1
  0.7 0.0 copy-start.2
  0.7 0.0 copy-start.3
  0.7 25.3 %tile_step.1 = (bf16[576,1280]{1,0:T(8,128)(2,1)S(1)}, bf16[576,1280]{1,0:T(8,128)(2,1)S(1)}, bf16[1152,1280]{1,0:T(8,128)(2,1)S(1)}, bf16[1152,1280]{1,0:T(8,128)(2,1)S(1)}) custom-call(s32[2,16]{1,0:T(2,128)S(1)} %bitcast.1, f32[2,576,576]{2,1,0:T(8,128)} %tiles_in.1, f32[2,128,128]{2,1,0:T(8,128)} %pupils_in.1, f32[16,128,128]{2,1,0:T(8,128)} %intensity_in.1, ...), custom_call_target="tpu_custom_call" | custom-call | tf_op jit(solution)/shard_map/tile_step/pallas_call | solution.py:373
  26.0 0.0 copy-done
  26.0 0.0 copy-done.1
  26.0 0.0 copy-done.2
  26.1 0.0 copy-done.3
  26.1 100.6 %field_step.1 = f32[2,512,512]{2,1,0:T(8,128)S(1)} custom-call(bf16[576,1280]{1,0:T(8,128)(2,1)S(1)} %get-tuple-element.9.l_hi, bf16[576,1280]{1,0:T(8,128)(2,1)S(1)} %get-tuple-element.10.l_lo, bf16[1152,1280]{1,0:T(8,128)(2,1)S(1)} %get-tuple-element.11.v_hi, bf16[1152,1280]{1,0:T(8,128)(2,1)S(1)} %get-tuple-element.12.v_lo, f32[4,32,128]{2,1,0:T(8,128)S(1)} %copy-done.3, ...), custom_call_target="tpu_custom_call" | custom-call | tf_op jit(solution)/shard_map/field_step/pallas_call | solution.py:781
  126.7 1.3 %copy.15 = f32[2,512,512]{2,1,0:T(8,128)} copy(f32[2,512,512]{2,1,0:T(8,128)S(1)} %field_step.1) | data formatting | bytes 4194304
Async XLA Ops:
  0.0 0.7 copy-start.4
  0.7 25.4 %copy-start = (bf16[4,256,256]{2,1,0:T(8,128)(2,1)S(1)}, bf16[4,256,256]{2,1,0:T(8,128)(2,1)}, u32[]{:S(2)}) copy-start(bf16[4,256,256]{2,1,0:T(8,128)(2,1)} %constant.26.clone.c_mats) | copy-start | bytes 1572868
  0.7 25.4 %copy-start.1 = (bf16[4,256,256]{2,1,0:T(8,128)(2,1)S(1)}, bf16[4,256,256]{2,1,0:T(8,128)(2,1)}, u32[]{:S(2)}) copy-start(bf16[4,256,256]{2,1,0:T(8,128)(2,1)} %constant.24.clone.r_mats) | copy-start | bytes 1572868
  0.7 25.4 %copy-start.2 = (f32[4,128,128]{2,1,0:T(8,128)S(1)}, f32[4,128,128]{2,1,0:T(8,128)}, u32[]{:S(2)}) copy-start(f32[4,128,128]{2,1,0:T(8,128)} %constant.25.clone.c_rows) | copy-start | bytes 786436
  0.7 25.4 %copy-start.3 = (f32[4,32,128]{2,1,0:T(8,128)S(1)}, f32[4,32,128]{2,1,0:T(8,128)}, u32[]{:S(2)}) copy-start(f32[4,32,128]{2,1,0:T(8,128)} %constant.23.clone.r_rows) | copy-start | bytes 196612

commit v4 on v3

--- a/solution.py
+++ b/solution.py
@@ -147,9 +147,7 @@
     forward = np.stack(split_np(np.stack(forward)))
     inverse = np.stack(split_np(np.stack(inverse)))
     window = dft_np(WIN, -1) / math.sqrt(WIN)
-    lanes = np.stack(
-        [*split_np(right_block(np.conj(window))), *split_np(right_block(window))]
-    )
+    lanes = np.stack(split_np(right_block(np.conj(window))))
     sides = np.stack(
         [*split_np(left_block(np.conj(window))), *split_np(left_block(window))]
     )
@@ -181,15 +179,17 @@
 
 
 def tile_body(
-    offs, tiles_in, pupils_in, intensity_in, seeds_in, fwd_in, inv_in, lanes_in, sides_in, l_hi, l_lo, v_hi, v_lo,
-    base, t_hi, t_lo, x_hi, x_lo, y, sub, spec, new, win_a, win_b,
-    tiles, pupils, intensity, seeds, fwd, inv, lanes, sides, sems,
+    offs, tiles_in, pupils_in, intensity_in, seeds_in, fwd_in, inv_in, lanes_in, sides_in,
+    z_hi, z_lo, r_hi, r_lo,
+    base, y, sub, spec, new, win_a, win_b, turned,
+    tiles, raw, pupils, intensity, seeds, fwd, inv, lanes, sides, sems,
 ):
-    sources = (seeds_in, tiles_in, fwd_in, pupils_in, intensity_in, lanes_in, sides_in, inv_in)
-    targets = (seeds, tiles, fwd, pupils, intensity, lanes, sides, inv)
+    pairs = [(seeds_in, seeds), (tiles_in, raw), (fwd_in, fwd)]
+    pairs += [(pupils_in, pupils), (intensity_in, intensity)]
+    pairs += [(lanes_in, lanes), (sides_in, sides), (inv_in, inv)]
     loads = [
         pltpu.make_async_copy(source, target, sems.at[index])
-        for index, (source, target) in enumerate(zip(sources, targets))
+        for index, (source, target) in enumerate(pairs)
     ]
     for load in loads:
         load.start()
@@ -206,119 +206,124 @@
         base[0, pl.ds(start, 24), :] = tr
         base[1, pl.ds(start, 24), :] = ti
 
-    zero_tail = jnp.zeros((PAD - TILE, 2 * PAD), BF)
-    t_hi[TILE:PAD, :] = zero_tail
-    t_lo[TILE:PAD, :] = zero_tail
-    t_hi[PAD + TILE :, :] = zero_tail
-    t_lo[PAD + TILE :, :] = zero_tail
+    for ref in (r_hi, r_lo):
+        zero_tail = jnp.zeros((PAD - TILE, 2 * TILE), BF)
+        ref[TILE:PAD, :] = zero_tail
+        ref[PAD + TILE :, :] = zero_tail
 
     @pl.loop(0, TILE // 96)
     def _(a):
         start = pl.multiple_of(a * 96, 16)
-        ch, cl = split(base[0, pl.ds(start, 96), :])
-        sh, sl = split(base[1, pl.ds(start, 96), :])
-        t_hi[pl.ds(start, 96), :PAD] = ch
-        t_lo[pl.ds(start, 96), :PAD] = cl
-        t_hi[pl.ds(start, 96), PAD:] = sh
-        t_lo[pl.ds(start, 96), PAD:] = sl
-        l_hi[pl.ds(start, 96), :PAD] = ch
-        l_lo[pl.ds(start, 96), :PAD] = cl
-        l_hi[pl.ds(start, 96), PAD:] = sh
-        l_lo[pl.ds(start, 96), PAD:] = sl
-        t_hi[pl.ds(start + PAD, 96), :PAD] = -sh
-        t_lo[pl.ds(start + PAD, 96), :PAD] = -sl
-        t_hi[pl.ds(start + PAD, 96), PAD:] = ch
-        t_lo[pl.ds(start + PAD, 96), PAD:] = cl
+        re, im = base[0, pl.ds(start, 96), :], base[1, pl.ds(start, 96), :]
+        for offset, left, right in ((0, re, -im), (PAD, im, re)):
+            at = pl.ds(start + offset, 96)
+            ends = left[:, STRIDE:] + pltpu.roll(right[:, STRIDE:], 64, 1)
+            for where, value in (
+                (slice(0, STRIDE), left[:, :STRIDE]),
+                (slice(STRIDE, 2 * STRIDE), right[:, :STRIDE]),
+                (slice(2 * STRIDE, 2 * TILE), ends),
+            ):
+                high, low = split(value)
+                r_hi[at, where] = high
+                r_lo[at, where] = low
+
+    def forward(targets):
+        @pl.loop(0, RADIX)
+        def _(b):
+            rows = pl.ds(b, SUB, stride=RADIX)
+            parts = [
+                jnp.concatenate([tiles[part, n, rows, :] for n in range(5)], axis=1)
+                for part in range(2)
+            ]
+            sub[b] = mm3((fwd[0, b], fwd[1, b]), split(jnp.concatenate(parts, axis=0)))
+
+        @pl.loop(0, PAD // 128)
+        def _(n):
+            at = pl.ds(pl.multiple_of(n * 128, 128), 128)
+            for row in range(0, SUB, 8):
+                items = [
+                    (sub[b, row : row + 8, at], sub[b, SUB + row : SUB + row + 8, at])
+                    for b in range(RADIX)
+                ]
+                done = fft_list(items, -1)
+                for k in range(RADIX):
+                    here = slice(k * SUB + row, k * SUB + row + 8)
+                    for ref in targets:
+                        ref[0, here, at] = done[k][0]
+                        ref[1, here, at] = done[k][1]
 
     loads[1].wait()
-    x_hi[...] = jnp.zeros_like(x_hi)
-    x_lo[...] = jnp.zeros_like(x_lo)
-
-    @pl.loop(0, TILE // 96)
-    def _(a):
-        start = pl.multiple_of(a * 96, 16)
-        for part in range(2):
-            high, low = split(tiles[part, pl.ds(start, 96), :])
-            x_hi[pl.ds(start, 96), part * PAD : part * PAD + TILE] = high
-            x_lo[pl.ds(start, 96), part * PAD : part * PAD + TILE] = low
-
-    @pl.loop(0, 2 * PAD // 256)
-    def _(n):
-        at = pl.ds(pl.multiple_of(n * 256, 256), 256)
-        both = mm3((x_hi[...], x_lo[...]), (t_hi[:, at], t_lo[:, at]))
-        y[2 * n] = both[:, :128]
-        y[2 * n + 1] = both[:, 128:]
-
+    for part in range(2):
+        for n in range(5):
+            width = min(128, TILE - 128 * n)
+            tiles[part, n, :, :width] = raw[part, :, 128 * n : 128 * n + width]
     loads[2].wait()
-
-    @pl.loop(0, RADIX)
-    def _(b):
-        rows = pl.ds(b, SUB, stride=RADIX)
-        parts = [
-            jnp.concatenate([y[n, rows, :] for n in range(5 * part, 5 * part + 5)], axis=1)
-            for part in range(2)
-        ]
-        sub[b] = mm3((fwd[0, b], fwd[1, b]), split(jnp.concatenate(parts, axis=0)))
-
-    @pl.loop(0, PAD // 128)
-    def _(n):
-        at = pl.ds(pl.multiple_of(n * 128, 128), 128)
-        for row in range(0, SUB, 8):
-            items = [
-                (sub[b, row : row + 8, at], sub[b, SUB + row : SUB + row + 8, at])
-                for b in range(RADIX)
-            ]
-            done = fft_list(items, -1)
-            for k in range(RADIX):
-                here = slice(k * SUB + row, k * SUB + row + 8)
-                spec[0, here, at] = done[k][0]
-                spec[1, here, at] = done[k][1]
-                new[0, here, at] = done[k][0]
-                new[1, here, at] = done[k][1]
+    forward((spec,))
+
+    def flip(part, at, count, to):
+        for i in range(4):
+            block = jnp.transpose(spec[part, 128 * i : 128 * i + 128, at])
+            tiles[part, i, to, :] = block[:count]
+        half = jnp.concatenate([spec[part, STRIDE:TILE, at], jnp.zeros((64, 128), F32)], axis=0)
+        tiles[part, 4, to, :] = jnp.transpose(half)[:count]
+
+    for part in range(2):
+        @pl.loop(0, 4)
+        def _(j):
+            at = pl.ds(pl.multiple_of(j * 128, 128), 128)
+            flip(part, at, 128, at)
+
+        flip(part, slice(STRIDE, PAD), 64, slice(STRIDE, TILE))
+
+    forward((spec, new))
 
     for ref in (spec, new):
         for part in range(2):
             ref[part, TILE:, :] = jnp.zeros((8, PAD), F32)
     for load in loads[3:]:
         load.wait()
-    pr, pi = pupils[0], pupils[1]
+    for part in range(2):
+        turned[part] = jnp.transpose(pupils[part])
     inv_lanes = (lanes[0], lanes[1])
-    fwd_lanes = (lanes[2], lanes[3])
     inv_sides = (sides[0], sides[1])
     fwd_sides = (sides[2], sides[3])
 
+    def sides_nt(table, value):
+        high, low = split(value)
+        return mm_nt(table[0], high) + (mm_nt(table[1], high) + mm_nt(table[0], low))
+
+    def restack(value):
+        for j in range(GROUP):
+            win_b[j * WIN : (j + 1) * WIN, :WIN] = value[:WIN, j * WIN : (j + 1) * WIN]
+            win_b[j * WIN : (j + 1) * WIN, WIN:] = value[WIN:, j * WIN : (j + 1) * WIN]
+
     @pl.loop(0, LEDS // GROUP)
     def _(step):
+        pr, pi = turned[0], turned[1]
         for j in range(GROUP):
             led = step * GROUP + j
-            row, col = offs[0, led], offs[1, led]
+            row, col = offs[1, led], offs[0, led]
             first = pl.multiple_of((col // 128) * 128, 128)
             shift = col - first
             back = lax.rem(256 - shift, 256)
             cr = cut(spec, 0, row, first, back)
             ci = cut(spec, 1, row, first, back)
             wr, wi = cmul(pr, pi, cr, ci)
-            win_a[:WIN, j * WIN : (j + 1) * WIN] = wr
-            win_a[WIN:, j * WIN : (j + 1) * WIN] = wi
-        side = mm3(inv_sides, split(win_a[...]))
-        for j in range(GROUP):
-            win_b[j * WIN : (j + 1) * WIN, :WIN] = side[:WIN, j * WIN : (j + 1) * WIN]
-            win_b[j * WIN : (j + 1) * WIN, WIN:] = side[WIN:, j * WIN : (j + 1) * WIN]
+            win_b[j * WIN : (j + 1) * WIN, :WIN] = wr
+            win_b[j * WIN : (j + 1) * WIN, WIN:] = wi
+        restack(sides_nt(inv_sides, win_b[...]))
         wave = mm3(split(win_b[...]), inv_lanes)
         for j in range(GROUP):
             wr = wave[j * WIN : (j + 1) * WIN, :WIN]
             wi = wave[j * WIN : (j + 1) * WIN, WIN:]
             excess = wr * wr + wi * wi - intensity[step * GROUP + j]
-            win_b[j * WIN : (j + 1) * WIN, :WIN] = wr * excess
-            win_b[j * WIN : (j + 1) * WIN, WIN:] = wi * excess
-        grad = mm3(split(win_b[...]), fwd_lanes)
-        for j in range(GROUP):
-            win_a[:WIN, j * WIN : (j + 1) * WIN] = grad[j * WIN : (j + 1) * WIN, :WIN]
-            win_a[WIN:, j * WIN : (j + 1) * WIN] = grad[j * WIN : (j + 1) * WIN, WIN:]
-        win_a[...] = mm3(fwd_sides, split(win_a[...]))
+            win_a[:WIN, j * WIN : (j + 1) * WIN] = wr * excess
+            win_a[WIN:, j * WIN : (j + 1) * WIN] = wi * excess
+        restack(mm3(fwd_sides, split(win_a[...])))
+        win_a[...] = sides_nt(fwd_sides, win_b[...])
         for j in range(GROUP):
             led = step * GROUP + j
-            row, col = offs[0, led], offs[1, led]
+            row, col = offs[1, led], offs[0, led]
             first = pl.multiple_of((col // 128) * 128, 128)
             shift = col - first
             gr = win_a[:WIN, j * WIN : (j + 1) * WIN] * -STEP_SIZE
@@ -348,20 +353,11 @@
             y[n, rows, :] = mixed[:SUB, 128 * n : 128 * n + 128]
             y[5 + n, rows, :] = mixed[SUB:, 128 * n : 128 * n + 128]
 
-    def put(start, count, real_at, imag_at):
-        for n in range(5):
-            rh, rl = split(y[n, start : start + count, :])
-            ih, il = split(y[5 + n, start : start + count, :])
-            left, right = slice(128 * n, 128 * n + 128), slice(PAD + 128 * n, PAD + 128 * n + 128)
-            a = slice(real_at, real_at + count)
-            v_hi[a, left], v_hi[a, right] = rh, ih
-            v_lo[a, left], v_lo[a, right] = rl, il
-            b = slice(imag_at, imag_at + count)
-            v_hi[b, left], v_hi[b, right] = ih, -rh
-            v_lo[b, left], v_lo[b, right] = il, -rl
-
-    put(0, STRIDE, 0, STRIDE)
-    put(STRIDE, OVL, 2 * STRIDE, 2 * STRIDE + OVL)
+    for n in range(10):
+        at = slice(128 * n, 128 * n + 128)
+        high, low = split(y[n])
+        z_hi[:, at] = high
+        z_lo[:, at] = low
 
 
 def vmem():
@@ -370,43 +366,39 @@
 
 def tile_step(tiles, pupils, intensity, offsets):
     seeds, fwd, inv, lanes, sides = tile_tables()
+    held = (pupils, intensity, seeds, fwd, inv, lanes, sides)
     return pl.pallas_call(
         tile_body,
         out_shape=[
             jax.ShapeDtypeStruct((TILE, 2 * PAD), BF),
             jax.ShapeDtypeStruct((TILE, 2 * PAD), BF),
-            jax.ShapeDtypeStruct((2 * TILE, 2 * PAD), BF),
-            jax.ShapeDtypeStruct((2 * TILE, 2 * PAD), BF),
+            jax.ShapeDtypeStruct((2 * PAD, 2 * TILE), BF),
+            jax.ShapeDtypeStruct((2 * PAD, 2 * TILE), BF),
         ],
         in_specs=[pl.BlockSpec(memory_space=pltpu.SMEM)]
         + [pl.BlockSpec(memory_space=pltpu.HBM)] * 8,
         out_specs=[vmem()] * 4,
         scratch_shapes=[
             pltpu.VMEM((2, TILE, PAD), F32),
-            pltpu.VMEM((2 * PAD, 2 * PAD), BF),
-            pltpu.VMEM((2 * PAD, 2 * PAD), BF),
-            pltpu.VMEM((TILE, 2 * PAD), BF),
-            pltpu.VMEM((TILE, 2 * PAD), BF),
             pltpu.VMEM((2 * PAD // 128, TILE, 128), F32),
             pltpu.VMEM((RADIX, 2 * SUB, PAD), F32),
             pltpu.VMEM((2, TILE + 8, PAD), F32),
             pltpu.VMEM((2, TILE + 8, PAD), F32),
             pltpu.VMEM((2 * WIN, GROUP * WIN), F32),
             pltpu.VMEM((GROUP * WIN, 2 * WIN), F32),
-            *[
-                pltpu.VMEM(value.shape, value.dtype)
-                for value in (tiles, pupils, intensity, seeds, fwd, inv, lanes, sides)
-            ],
+            pltpu.VMEM((2, WIN, WIN), F32),
+            pltpu.VMEM((2, PAD // 128, TILE, 128), F32),
+            pltpu.VMEM((2, TILE, TILE), F32),
+            *[pltpu.VMEM(value.shape, value.dtype) for value in held],
             pltpu.SemaphoreType.DMA((8,)),
         ],
         compiler_params=pltpu.CompilerParams(vmem_limit_bytes=A_LIMIT << 20),
         name="tile_step",
     )(
-        offsets,
         *[
             pltpu.with_memory_space_constraint(jnp.asarray(value), pltpu.HBM)
-            for value in (tiles, pupils, intensity, seeds, fwd, inv, lanes, sides)
-        ],
+            for value in (offsets, tiles, *held)
+        ]
     )
 
 
@@ -450,9 +442,9 @@
 
 
 def field_body(
-    l_hi, l_lo, v_hi, v_lo, r_rows, r_mats, c_rows, c_mats, out,
+    z_hi, z_lo, r_hi, r_lo, r_rows, r_mats, c_rows, c_mats, out,
     refined, halo, front, got, work, mid, give, have, send,
-    halo_sem, send_sem, recv_row, own_row, recv_all, own_all, recv_col, own_sem,
+    halo_sem, send_sem, recv_row, own_row, recv_all, own_all, recv_col, own_sem, ready,
 ):
     row, col = lax.axis_index("row"), lax.axis_index("col")
     xh, z = row // 4, lax.rem(row, 4)
@@ -461,12 +453,10 @@
     cols_at = [lax.rem(col + step, 16) for step in range(16)]
 
     barrier = pltpu.get_barrier_semaphore()
-    for i in range(8):
-        for j in range(16):
-            if i or j:
-                pl.semaphore_signal(
-                    barrier, inc=1, device_id=(rows_at[i], cols_at[j]), device_id_type=MESH
-                )
+    for i in range(1, 8):
+        pl.semaphore_signal(barrier, inc=1, device_id=(rows_at[i], col), device_id_type=MESH)
+    for j in range(1, 16):
+        pl.semaphore_signal(barrier, inc=1, device_id=(row, cols_at[j]), device_id_type=MESH)
 
     chunks = [lax.rem(xh + i, 2) * 4 + lax.rem(z + j, 4) for i, j in FAR_ROWS]
 
@@ -474,10 +464,9 @@
         places = [pl.ds(pl.multiple_of(block * 64, 64), 64) for block in blocks]
 
         def fill(at):
-            high = jnp.concatenate([l_hi[place, :] for place in places], axis=0)
-            low = jnp.concatenate([l_lo[place, :] for place in places], axis=0)
-            righl_high, righl_low = v_hi[at, :], v_lo[at, :]
-            value = mm_nt(high, righl_high) + (mm_nt(low, righl_high) + mm_nt(high, righl_low))
+            high = jnp.concatenate([z_hi[place, :] for place in places], axis=0)
+            low = jnp.concatenate([z_lo[place, :] for place in places], axis=0)
+            value = mm3((high, low), (r_hi[:, at], r_lo[:, at]))
             for index, place in enumerate(places):
                 refined[place, at] = value[64 * index : 64 * index + 64]
 
@@ -488,7 +477,9 @@
         fill(slice(1024, 1152))
 
     columns_of([8, *chunks[:2]])
-    pl.semaphore_wait(barrier, 127)
+    pl.semaphore_wait(barrier, 22)
+    for j in range(1, 16):
+        pl.semaphore_signal(ready, inc=1, device_id=(row, cols_at[j]), device_id_type=MESH)
 
     edge = pltpu.make_async_remote_copy(
         refined.at[STRIDE:], halo, halo_sem.at[0], halo_sem.at[1],
@@ -509,37 +500,35 @@
     def blended(quarter):
         return front.at[quarter * QUARTER : (quarter + 1) * QUARTER]
 
-    def give_plain(targets):
+    def give_plain(targets, quarter=0):
         for target in targets:
             @pl.when(target != 0)
             def _():
-                give_row(target, 0, plain(target, 0))
+                give_row(target, quarter, plain(target, quarter))
+
+    def give_blended(quarter):
+        for target in chunks:
+            @pl.when(target == 0)
+            def _():
+                give_row(target, quarter, blended(quarter))
 
     give_plain(chunks[:2])
     columns_of(chunks[2:5])
     give_plain(chunks[2:5])
     columns_of([*chunks[5:], row])
     give_plain(chunks[5:])
+    give_plain(chunks, 1)
 
     edge.wait()
     place = lax.broadcasted_iota(jnp.int32, (OVL, 2 * TILE), 0).astype(F32)
     ramp = (place + 0.5) / OVL
     front[...] = ramp * refined[:OVL] + (1.0 - ramp) * halo[...]
 
-    for target in chunks:
-        @pl.when(target == 0)
-        def _():
-            give_row(target, 0, blended(0))
-
-    for quarter in range(1, 4):
-        for target in chunks:
-            @pl.when(target != 0)
-            def _():
-                give_row(target, quarter, plain(target, quarter))
-
-            @pl.when(target == 0)
-            def _():
-                give_row(target, quarter, blended(quarter))
+    give_blended(0)
+    give_blended(1)
+    for quarter in range(2, 4):
+        give_plain(chunks, quarter)
+        give_blended(quarter)
 
     @pl.when(row == 0)
     def _():
@@ -655,6 +644,8 @@
             else:
                 pl.when(step != own_step)(go)
 
+    pl.semaphore_wait(ready, 15)
+
     @pl.loop(0, 32)
     def _(step):
         block, ends = peers(step)
@@ -775,7 +766,7 @@
     settle(send.at[:15], send_sem.at[2])
 
 
-def field_step(l_hi, l_lo, v_hi, v_lo):
+def field_step(z_hi, z_lo, r_hi, r_lo):
     r_rows, r_mats = row_tables()
     c_rows, c_mats, _ = col_tables()
     return pl.pallas_call(
@@ -801,12 +792,13 @@
             pltpu.SemaphoreType.DMA(()),
             pltpu.SemaphoreType.DMA((2,)),
             pltpu.SemaphoreType.DMA((2,)),
+            pltpu.SemaphoreType.REGULAR,
         ],
         compiler_params=pltpu.CompilerParams(
             vmem_limit_bytes=B_LIMIT << 20, collective_id=0, has_side_effects=True
         ),
         name="field_step",
-    )(l_hi, l_lo, v_hi, v_lo, r_rows, r_mats, c_rows, c_mats)
+    )(z_hi, z_lo, r_hi, r_lo, r_rows, r_mats, c_rows, c_mats)
 
 
 def local(tiles, pupils, intensity, offsets):

time: 128 us -> 120 us (0.938)
  the two profiles are of different devices: /device:TPU:31 before, /device:TPU:1 now
where the time goes in v4:
time: 120 us; the launch traced here: 119 us
  Pallas kernels  118 us (98%)
  local copies, waits for them, and re-layouts  1.34 us (1%)
    pallas_call x1, Pallas kernels, field_step(): pl.pallas_call(field_body, out_shape=jax.ShapeDtypeStruct((2, STRIDE, STR...  94.7 us
    pallas_call x1, Pallas kernels, tile_step(): pl.pallas_call(tile_body, out_shape=[jax.ShapeDtypeStruct((TILE, 2 * PAD)...  23.1 us

profile of v4, /device:TPU:1, one launch (start us, length us, event | category | flops | bytes accessed | tf_op | source)
XLA Modules:
  0.0 119.2 jit_solution(5760594251302996633)
XLA Ops:
  0.0 0.0 copy-start
  0.0 0.0 copy-start.1
  0.0 0.0 copy-start.2
  0.0 0.0 copy-start.3
  0.0 23.1 %tile_step.1 = (bf16[576,1280]{1,0:T(8,128)(2,1)S(1)}, bf16[576,1280]{1,0:T(8,128)(2,1)S(1)}, bf16[1280,1152]{1,0:T(8,128)(2,1)S(1)}, bf16[1280,1152]{1,0:T(8,128)(2,1)S(1)}) custom-call(s32[2,16]{1,0:T(2,128)} %bitcast.1, f32[2,576,576]{2,1,0:T(8,128)} %tiles_in.1, f32[2,128,128]{2,1,0:T(8,128)} %pupils_in.1, f32[16,128,128]{2,1,0:T(8,128)} %intensity_in.1, ...), custom_call_target="tpu_custom_call" | custom-call | tf_op jit(solution)/shard_map/tile_step/pallas_call | solution.py:370
  23.1 0.0 copy-done
  23.1 0.0 copy-done.1
  23.1 0.0 copy-done.2
  23.1 0.0 copy-done.3
  23.1 94.7 %field_step.1 = f32[2,512,512]{2,1,0:T(8,128)S(1)} custom-call(bf16[576,1280]{1,0:T(8,128)(2,1)S(1)} %get-tuple-element.9.z_hi, bf16[576,1280]{1,0:T(8,128)(2,1)S(1)} %get-tuple-element.10.z_lo, bf16[1280,1152]{1,0:T(8,128)(2,1)S(1)} %get-tuple-element.11.r_hi, bf16[1280,1152]{1,0:T(8,128)(2,1)S(1)} %get-tuple-element.12.r_lo, f32[4,32,128]{2,1,0:T(8,128)S(1)} %copy-done.3, ...), custom_call_target="tpu_custom_call" | custom-call | tf_op jit(solution)/shard_map/field_step/pallas_call | solution.py:772
  117.8 1.3 %copy.15 = f32[2,512,512]{2,1,0:T(8,128)} copy(f32[2,512,512]{2,1,0:T(8,128)S(1)} %field_step.1) | data formatting | bytes 4194304
Async XLA Ops:
  0.0 23.1 %copy-start = (bf16[4,256,256]{2,1,0:T(8,128)(2,1)S(1)}, bf16[4,256,256]{2,1,0:T(8,128)(2,1)}, u32[]{:S(2)}) copy-start(bf16[4,256,256]{2,1,0:T(8,128)(2,1)} %constant.26.clone.c_mats) | copy-start | bytes 1572868
  0.0 23.1 %copy-start.1 = (bf16[4,256,256]{2,1,0:T(8,128)(2,1)S(1)}, bf16[4,256,256]{2,1,0:T(8,128)(2,1)}, u32[]{:S(2)}) copy-start(bf16[4,256,256]{2,1,0:T(8,128)(2,1)} %constant.24.clone.r_mats) | copy-start | bytes 1572868
  0.0 23.1 %copy-start.2 = (f32[4,128,128]{2,1,0:T(8,128)S(1)}, f32[4,128,128]{2,1,0:T(8,128)}, u32[]{:S(2)}) copy-start(f32[4,128,128]{2,1,0:T(8,128)} %constant.25.clone.c_rows) | copy-start | bytes 786436
  0.0 23.1 %copy-start.3 = (f32[4,32,128]{2,1,0:T(8,128)S(1)}, f32[4,32,128]{2,1,0:T(8,128)}, u32[]{:S(2)}) copy-start(f32[4,32,128]{2,1,0:T(8,128)} %constant.23.clone.r_rows) | copy-start | bytes 196612

commit v5 on v4

--- a/solution.py
+++ b/solution.py
@@ -23,7 +23,7 @@
 SUB = TILE // RADIX
 BF = jnp.bfloat16
 F32 = jnp.float32
-GROUP = 4
+GROUP = 8
 A_LIMIT = 38
 B_LIMIT = 24
 
@@ -181,7 +181,7 @@
 def tile_body(
     offs, tiles_in, pupils_in, intensity_in, seeds_in, fwd_in, inv_in, lanes_in, sides_in,
     z_hi, z_lo, r_hi, r_lo,
-    base, y, sub, spec, new, win_a, win_b, turned,
+    base, y, sub, spec, wins_a, wins_b, turned,
     tiles, raw, pupils, intensity, seeds, fwd, inv, lanes, sides, sems,
 ):
     pairs = [(seeds_in, seeds), (tiles_in, raw), (fwd_in, fwd)]
@@ -227,7 +227,7 @@
                 r_hi[at, where] = high
                 r_lo[at, where] = low
 
-    def forward(targets):
+    def forward():
         @pl.loop(0, RADIX)
         def _(b):
             rows = pl.ds(b, SUB, stride=RADIX)
@@ -248,9 +248,8 @@
                 done = fft_list(items, -1)
                 for k in range(RADIX):
                     here = slice(k * SUB + row, k * SUB + row + 8)
-                    for ref in targets:
-                        ref[0, here, at] = done[k][0]
-                        ref[1, here, at] = done[k][1]
+                    spec[0, here, at] = done[k][0]
+                    spec[1, here, at] = done[k][1]
 
     loads[1].wait()
     for part in range(2):
@@ -258,7 +257,7 @@
             width = min(128, TILE - 128 * n)
             tiles[part, n, :, :width] = raw[part, :, 128 * n : 128 * n + width]
     loads[2].wait()
-    forward((spec,))
+    forward()
 
     def flip(part, at, count, to):
         for i in range(4):
@@ -275,11 +274,10 @@
 
         flip(part, slice(STRIDE, PAD), 64, slice(STRIDE, TILE))
 
-    forward((spec, new))
-
-    for ref in (spec, new):
-        for part in range(2):
-            ref[part, TILE:, :] = jnp.zeros((8, PAD), F32)
+    forward()
+
+    for part in range(2):
+        spec[part, TILE:, :] = jnp.zeros((8, PAD), F32)
     for load in loads[3:]:
         load.wait()
     for part in range(2):
@@ -292,26 +290,29 @@
         high, low = split(value)
         return mm_nt(table[0], high) + (mm_nt(table[1], high) + mm_nt(table[0], low))
 
-    def restack(value):
+    def restack(win_b, value):
         for j in range(GROUP):
             win_b[j * WIN : (j + 1) * WIN, :WIN] = value[:WIN, j * WIN : (j + 1) * WIN]
             win_b[j * WIN : (j + 1) * WIN, WIN:] = value[WIN:, j * WIN : (j + 1) * WIN]
 
-    @pl.loop(0, LEDS // GROUP)
-    def _(step):
-        pr, pi = turned[0], turned[1]
+    pr, pi = turned[0], turned[1]
+    for step in range(LEDS // GROUP):
+        win_b = wins_b.at[step]
         for j in range(GROUP):
             led = step * GROUP + j
             row, col = offs[1, led], offs[0, led]
             first = pl.multiple_of((col // 128) * 128, 128)
-            shift = col - first
-            back = lax.rem(256 - shift, 256)
+            back = lax.rem(first + 256 - col, 256)
             cr = cut(spec, 0, row, first, back)
             ci = cut(spec, 1, row, first, back)
             wr, wi = cmul(pr, pi, cr, ci)
             win_b[j * WIN : (j + 1) * WIN, :WIN] = wr
             win_b[j * WIN : (j + 1) * WIN, WIN:] = wi
-        restack(sides_nt(inv_sides, win_b[...]))
+
+    for step in range(LEDS // GROUP):
+        win_a, win_b = wins_a.at[step], wins_b.at[step]
+        pr, pi = turned[0], turned[1]
+        restack(win_b, sides_nt(inv_sides, win_b[...]))
         wave = mm3(split(win_b[...]), inv_lanes)
         for j in range(GROUP):
             wr = wave[j * WIN : (j + 1) * WIN, :WIN]
@@ -319,7 +320,7 @@
             excess = wr * wr + wi * wi - intensity[step * GROUP + j]
             win_a[:WIN, j * WIN : (j + 1) * WIN] = wr * excess
             win_a[WIN:, j * WIN : (j + 1) * WIN] = wi * excess
-        restack(mm3(fwd_sides, split(win_a[...])))
+        restack(win_b, mm3(fwd_sides, split(win_a[...])))
         win_a[...] = sides_nt(fwd_sides, win_b[...])
         for j in range(GROUP):
             led = step * GROUP + j
@@ -329,8 +330,8 @@
             gr = win_a[:WIN, j * WIN : (j + 1) * WIN] * -STEP_SIZE
             gi = win_a[WIN:, j * WIN : (j + 1) * WIN] * -STEP_SIZE
             ur, ui = cmul(pr, -pi, gr, gi)
-            add(new, 0, row, first, shift, ur)
-            add(new, 1, row, first, shift, ui)
+            add(spec, 0, row, first, shift, ur)
+            add(spec, 1, row, first, shift, ui)
 
     @pl.loop(0, PAD // 128)
     def _(n):
@@ -339,7 +340,7 @@
             items = []
             for k in range(RADIX):
                 here = slice(k * SUB + row, k * SUB + row + 8)
-                items.append((new[0, here, at], new[1, here, at]))
+                items.append((spec[0, here, at], spec[1, here, at]))
             done = fft_list(items, 1)
             for b in range(RADIX):
                 sub[b, row : row + 8, at] = done[b][0]
@@ -383,9 +384,8 @@
             pltpu.VMEM((2 * PAD // 128, TILE, 128), F32),
             pltpu.VMEM((RADIX, 2 * SUB, PAD), F32),
             pltpu.VMEM((2, TILE + 8, PAD), F32),
-            pltpu.VMEM((2, TILE + 8, PAD), F32),
-            pltpu.VMEM((2 * WIN, GROUP * WIN), F32),
-            pltpu.VMEM((GROUP * WIN, 2 * WIN), F32),
+            pltpu.VMEM((LEDS // GROUP, 2 * WIN, GROUP * WIN), F32),
+            pltpu.VMEM((LEDS // GROUP, GROUP * WIN, 2 * WIN), F32),
             pltpu.VMEM((2, WIN, WIN), F32),
             pltpu.VMEM((2, PAD // 128, TILE, 128), F32),
             pltpu.VMEM((2, TILE, TILE), F32),
@@ -434,7 +434,7 @@
     ((y, x, k) for y in range(4) for x in range(2) for k in range(2) if y or x or k),
     key=lambda step: -(min(step[0], 4 - step[0]) + step[1]),
 )
-QUARTER = 16
+QUARTER = 8
 
 
 def settle(ref, sem):
@@ -517,16 +517,17 @@
     give_plain(chunks[2:5])
     columns_of([*chunks[5:], row])
     give_plain(chunks[5:])
-    give_plain(chunks, 1)
+    for quarter in range(1, 4):
+        give_plain(chunks, quarter)
 
     edge.wait()
     place = lax.broadcasted_iota(jnp.int32, (OVL, 2 * TILE), 0).astype(F32)
     ramp = (place + 0.5) / OVL
     front[...] = ramp * refined[:OVL] + (1.0 - ramp) * halo[...]
 
-    give_blended(0)
-    give_blended(1)
-    for quarter in range(2, 4):
+    for quarter in range(4):
+        give_blended(quarter)
+    for quarter in range(4, 8):
         give_plain(chunks, quarter)
         give_blended(quarter)
 
@@ -545,77 +546,73 @@
     slope = jnp.where(lane < OVL, (lane.astype(F32) + 0.5) / OVL, 1.0)
     rest = jnp.where(lane < OVL, 1.0 - slope, 0.0)
 
-    @pl.loop(0, 4)
+    @pl.loop(0, 8)
     def _(quarter):
         columns = pl.ds(pl.multiple_of(quarter * QUARTER, QUARTER), QUARTER)
         settle(got.at[:7, columns], recv_row.at[quarter])
 
-        @pl.loop(0, 2)
-        def _(half):
-            at = pl.ds(pl.multiple_of(quarter * QUARTER + half * 8, 8), 8)
-            for a in range(4):
-                items = []
-                for p in range(8):
-                    re = got[p, at, 128 * a : 128 * a + 128]
-                    im = got[p, at, STRIDE + 128 * a : STRIDE + 128 * a + 128]
-                    if a == 0:
-                        tail = got[(p - 1) % 8, at, 2 * STRIDE :]
-                        re = slope * re + rest * tail
-                        im = slope * im + rest * pltpu.roll(tail, 64, 1)
-                    items.append((re, im))
-                done = fft_list(items, -1)
-                for k in range(8):
-                    re, im = cscale(done[k], unit(-a * k / 32))
-                    mid[4 * k + a, 0, at, :] = re
-                    mid[4 * k + a, 1, at, :] = im
-
-            @pl.loop(0, 8)
-            def _(k):
-                items = [(mid[4 * k + a, 0, at, :], mid[4 * k + a, 1, at, :]) for a in range(4)]
-                done = fft_list(items, -1)
-                for q in range(4):
-                    index = k + 8 * q
-                    tr = r_rows[0, pl.ds(index, 1), :]
-                    ti = r_rows[1, pl.ds(index, 1), :]
-                    re, im = cmul(*done[q], tr, ti)
-                    start = pl.ds(pl.multiple_of(index * QUARTER + half * 8, 8), 8)
-                    work[start, :128] = re
-                    work[start, 128:] = im
-
-        full = mm3(split(work[:512]), (r_mats[0], r_mats[1]))
+        at = pl.ds(pl.multiple_of(quarter * QUARTER, 8), 8)
+        for a in range(4):
+            items = []
+            for p in range(8):
+                re = got[p, at, 128 * a : 128 * a + 128]
+                im = got[p, at, STRIDE + 128 * a : STRIDE + 128 * a + 128]
+                if a == 0:
+                    tail = got[(p - 1) % 8, at, 2 * STRIDE :]
+                    re = slope * re + rest * tail
+                    im = slope * im + rest * pltpu.roll(tail, 64, 1)
+                items.append((re, im))
+            done = fft_list(items, -1)
+            for k in range(8):
+                re, im = cscale(done[k], unit(-a * k / 32))
+                mid[4 * k + a, 0, at, :] = re
+                mid[4 * k + a, 1, at, :] = im
+
+        @pl.loop(0, 8)
+        def _(k):
+            items = [(mid[4 * k + a, 0, at, :], mid[4 * k + a, 1, at, :]) for a in range(4)]
+            done = fft_list(items, -1)
+            for q in range(4):
+                index = k + 8 * q
+                tr = r_rows[0, pl.ds(index, 1), :]
+                ti = r_rows[1, pl.ds(index, 1), :]
+                re, im = cmul(*done[q], tr, ti)
+                start = pl.ds(pl.multiple_of(index * QUARTER, 8), 8)
+                work[start, :128] = re
+                work[start, 128:] = im
+
+        full = mm3(split(work[:256]), (r_mats[0], r_mats[1]))
         full = full.reshape(32, QUARTER, 256)
         kr, ki = r_rows[2][:, None, :], r_rows[3][:, None, :]
         re, im = cmul(full[:, :, :128], full[:, :, 128:], kr, ki)
-        both = jnp.concatenate([re, im], axis=2).reshape(512, 256)
-        work[:512] = mm3(split(both), (r_mats[2], r_mats[3]))
-
-        @pl.loop(0, 2)
-        def _(half):
-            at = pl.ds(pl.multiple_of(quarter * QUARTER + half * 8, 8), 8)
-
-            @pl.loop(0, 8)
-            def _(k):
-                items = []
-                for q in range(4):
-                    index = k + 8 * q
-                    tr = r_rows[0, pl.ds(index, 1), :]
-                    ti = r_rows[1, pl.ds(index, 1), :]
-                    start = pl.ds(pl.multiple_of(index * QUARTER + half * 8, 8), 8)
-                    items.append(cmul(work[start, :128], work[start, 128:], tr, -ti))
-                done = fft_list(items, 1)
-                for a in range(4):
-                    mid[4 * k + a, 0, at, :] = done[a][0]
-                    mid[4 * k + a, 1, at, :] = done[a][1]
-
+        both = jnp.concatenate([re, im], axis=2).reshape(256, 256)
+        work[:256] = mm3(split(both), (r_mats[2], r_mats[3]))
+
+        at = pl.ds(pl.multiple_of(quarter * QUARTER, 8), 8)
+
+        @pl.loop(0, 8)
+        def _(k):
+            items = []
+            for q in range(4):
+                index = k + 8 * q
+                tr = r_rows[0, pl.ds(index, 1), :]
+                ti = r_rows[1, pl.ds(index, 1), :]
+                start = pl.ds(pl.multiple_of(index * QUARTER, 8), 8)
+                items.append(cmul(work[start, :128], work[start, 128:], tr, -ti))
+            done = fft_list(items, 1)
             for a in range(4):
-                items = [
-                    cscale((mid[4 * k + a, 0, at, :], mid[4 * k + a, 1, at, :]), unit(a * k / 32))
-                    for k in range(8)
-                ]
-                done = fft_list(items, 1)
-                for p in range(8):
-                    mid[4 * p + a, 0, at, :] = done[p][0]
-                    mid[4 * p + a, 1, at, :] = done[p][1]
+                mid[4 * k + a, 0, at, :] = done[a][0]
+                mid[4 * k + a, 1, at, :] = done[a][1]
+
+        for a in range(4):
+            items = [
+                cscale((mid[4 * k + a, 0, at, :], mid[4 * k + a, 1, at, :]), unit(a * k / 32))
+                for k in range(8)
+            ]
+            done = fft_list(items, 1)
+            for p in range(8):
+                mid[4 * p + a, 0, at, :] = done[p][0]
+                mid[4 * p + a, 1, at, :] = done[p][1]
 
     me = row * 16 + col
 
@@ -786,7 +783,7 @@
             pltpu.VMEM((16, 2, 32, STRIDE), F32),
             pltpu.SemaphoreType.DMA((2,)),
             pltpu.SemaphoreType.DMA((3,)),
-            pltpu.SemaphoreType.DMA((4,)),
+            pltpu.SemaphoreType.DMA((8,)),
             pltpu.SemaphoreType.DMA(()),
             pltpu.SemaphoreType.DMA((2,)),
             pltpu.SemaphoreType.DMA(()),

time: 120 us -> 118 us (0.983)
    pallas_call x1, Pallas kernels: 23.1 us -> 20.8 us  [tile_step(): pl.pallas_call(tile_body, out_shape=[jax.ShapeDtypeStruct((TILE, 2 * PAD)...]
    pallas_call x1, Pallas kernels: 94.7 us -> 96 us  [field_step(): pl.pallas_call(field_body, out_shape=jax.ShapeDtypeStruct((2, STRIDE, STR...]
where the time goes in v5:
time: 118 us
  Pallas kernels  117 us (99%)
  local copies, waits for them, and re-layouts  1.34 us (1%)
    pallas_call x1, Pallas kernels, field_step(): pl.pallas_call(field_body, out_shape=jax.ShapeDtypeStruct((2, STRIDE, STR...  96 us
    pallas_call x1, Pallas kernels, tile_step(): pl.pallas_call(tile_body, out_shape=[jax.ShapeDtypeStruct((TILE, 2 * PAD)...  20.8 us

profile of v5, /device:TPU:1, one launch (start us, length us, event | category | flops | bytes accessed | tf_op | source)
XLA Modules:
  0.0 118.3 jit_solution(16567202825544703694)
XLA Ops:
  0.0 0.0 copy-start
  0.0 0.0 copy-start.1
  0.0 0.0 copy-start.2
  0.0 0.0 copy-start.3
  0.0 20.8 %tile_step.1 = (bf16[576,1280]{1,0:T(8,128)(2,1)S(1)}, bf16[576,1280]{1,0:T(8,128)(2,1)S(1)}, bf16[1280,1152]{1,0:T(8,128)(2,1)S(1)}, bf16[1280,1152]{1,0:T(8,128)(2,1)S(1)}) custom-call(s32[2,16]{1,0:T(2,128)} %bitcast.1, f32[2,576,576]{2,1,0:T(8,128)} %tiles_in.1, f32[2,128,128]{2,1,0:T(8,128)} %pupils_in.1, f32[16,128,128]{2,1,0:T(8,128)} %intensity_in.1, ...), custom_call_target="tpu_custom_call" | custom-call | tf_op jit(solution)/shard_map/tile_step/pallas_call | solution.py:371
  20.9 0.0 copy-done
  20.9 0.0 copy-done.1
  20.9 0.0 copy-done.2
  20.9 0.0 copy-done.3
  20.9 96.0 %field_step.1 = f32[2,512,512]{2,1,0:T(8,128)S(1)} custom-call(bf16[576,1280]{1,0:T(8,128)(2,1)S(1)} %get-tuple-element.9.z_hi, bf16[576,1280]{1,0:T(8,128)(2,1)S(1)} %get-tuple-element.10.z_lo, bf16[1280,1152]{1,0:T(8,128)(2,1)S(1)} %get-tuple-element.11.r_hi, bf16[1280,1152]{1,0:T(8,128)(2,1)S(1)} %get-tuple-element.12.r_lo, f32[4,32,128]{2,1,0:T(8,128)S(1)} %copy-done.3, ...), custom_call_target="tpu_custom_call" | custom-call | tf_op jit(solution)/shard_map/field_step/pallas_call | solution.py:769
  117.0 1.3 %copy.15 = f32[2,512,512]{2,1,0:T(8,128)} copy(f32[2,512,512]{2,1,0:T(8,128)S(1)} %field_step.1) | data formatting | bytes 4194304
Async XLA Ops:
  0.0 20.9 %copy-start = (bf16[4,256,256]{2,1,0:T(8,128)(2,1)S(1)}, bf16[4,256,256]{2,1,0:T(8,128)(2,1)}, u32[]{:S(2)}) copy-start(bf16[4,256,256]{2,1,0:T(8,128)(2,1)} %constant.26.clone.c_mats) | copy-start | bytes 1572868
  0.0 20.9 %copy-start.1 = (bf16[4,256,256]{2,1,0:T(8,128)(2,1)S(1)}, bf16[4,256,256]{2,1,0:T(8,128)(2,1)}, u32[]{:S(2)}) copy-start(bf16[4,256,256]{2,1,0:T(8,128)(2,1)} %constant.24.clone.r_mats) | copy-start | bytes 1572868
  0.0 20.9 %copy-start.2 = (f32[4,128,128]{2,1,0:T(8,128)S(1)}, f32[4,128,128]{2,1,0:T(8,128)}, u32[]{:S(2)}) copy-start(f32[4,128,128]{2,1,0:T(8,128)} %constant.25.clone.c_rows) | copy-start | bytes 786436
  0.0 20.9 %copy-start.3 = (f32[4,32,128]{2,1,0:T(8,128)S(1)}, f32[4,32,128]{2,1,0:T(8,128)}, u32[]{:S(2)}) copy-start(f32[4,32,128]{2,1,0:T(8,128)} %constant.23.clone.r_rows) | copy-start | bytes 196612

commit v6 on v5

--- a/solution.py
+++ b/solution.py
@@ -685,14 +685,13 @@
                 work[flat : flat + 8, :128] = re
                 work[flat : flat + 8, 128:] = im
 
-        @pl.loop(0, 16)
-        def _(k):
-            places = [pl.ds(pl.multiple_of(8 * (16 * r + k), 8), 8) for r in range(8)]
+        for k in range(16):
+            places = [slice(8 * (16 * r + k), 8 * (16 * r + k) + 8) for r in range(8)]
             items = [(work[at, :128], work[at, 128:]) for at in places]
             done = fft_list(items, -1)
             for q in range(8):
-                tr = c_rows[0, pl.ds(16 * q + k, 1), :]
-                ti = c_rows[1, pl.ds(16 * q + k, 1), :]
+                tr = c_rows[0, 16 * q + k : 16 * q + k + 1, :]
+                ti = c_rows[1, 16 * q + k : 16 * q + k + 1, :]
                 re, im = cmul(*done[q], tr, ti)
                 work[places[q], :128] = re
                 work[places[q], 128:] = im
@@ -708,13 +707,12 @@
             both = jnp.concatenate([re, im], axis=2).reshape(512, 256)
             work[at, :] = mm3(split(both), (c_mats[2], c_mats[3]))
 
-        @pl.loop(0, 16)
-        def _(k):
-            places = [pl.ds(pl.multiple_of(8 * (16 * r + k), 8), 8) for r in range(8)]
+        for k in range(16):
+            places = [slice(8 * (16 * r + k), 8 * (16 * r + k) + 8) for r in range(8)]
             items = []
             for q in range(8):
-                tr = c_rows[0, pl.ds(16 * q + k, 1), :]
-                ti = c_rows[1, pl.ds(16 * q + k, 1), :]
+                tr = c_rows[0, 16 * q + k : 16 * q + k + 1, :]
+                ti = c_rows[1, 16 * q + k : 16 * q + k + 1, :]
                 items.append(cmul(work[places[q], :128], work[places[q], 128:], tr, -ti))
             done = fft_list(items, 1)
             for r in range(8):
@@ -733,8 +731,7 @@
                 work[flat : flat + 8, :128] = done[c][0]
                 work[flat : flat + 8, 128:] = done[c][1]
 
-        @pl.loop(0, 16)
-        def _(c):
+        def pack(c):
             for piece in range(2):
                 lanes = slice(128 * piece, 128 * piece + 128)
                 for pair in range(4):
@@ -749,10 +746,12 @@
         mine = pl.ds(pl.multiple_of(col * 32 + part * 16, 16), 16)
         for i, j, k in FAR_COLS:
             tc = lax.rem(y + i, 4) * 4 + lax.rem(xl + j, 2) * 2 + lax.rem(core + k, 2)
+            pack(tc)
             pltpu.make_async_remote_copy(
                 send.at[tc, :, lines], out.at[:, mine],
                 send_sem.at[2], recv_col.at[part], device_id=(row, tc), device_id_type=MESH,
             ).start()
+        pack(col)
         pltpu.make_async_copy(send.at[col, :, lines], out.at[:, mine], own_sem.at[part]).start()
 
     for part in range(2):

time: 118 us -> 117 us (level)
  no operation moved by 1% of the time
where the time goes in v6:
time: 117 us
  Pallas kernels  116 us (99%)
  local copies, waits for them, and re-layouts  1.34 us (1%)
    pallas_call x1, Pallas kernels, field_step(): pl.pallas_call(field_body, out_shape=jax.ShapeDtypeStruct((2, STRIDE, STR...  95 us
    pallas_call x1, Pallas kernels, tile_step(): pl.pallas_call(tile_body, out_shape=[jax.ShapeDtypeStruct((TILE, 2 * PAD)...  20.8 us

profile of v6, /device:TPU:1, one launch (start us, length us, event | category | flops | bytes accessed | tf_op | source)
XLA Modules:
  0.0 117.2 jit_solution(16904213174139666863)
XLA Ops:
  0.0 0.0 copy-start
  0.0 0.0 copy-start.1
  0.0 0.0 copy-start.2
  0.0 0.0 copy-start.3
  0.0 20.8 %tile_step.1 = (bf16[576,1280]{1,0:T(8,128)(2,1)S(1)}, bf16[576,1280]{1,0:T(8,128)(2,1)S(1)}, bf16[1280,1152]{1,0:T(8,128)(2,1)S(1)}, bf16[1280,1152]{1,0:T(8,128)(2,1)S(1)}) custom-call(s32[2,16]{1,0:T(2,128)} %bitcast.1, f32[2,576,576]{2,1,0:T(8,128)} %tiles_in.1, f32[2,128,128]{2,1,0:T(8,128)} %pupils_in.1, f32[16,128,128]{2,1,0:T(8,128)} %intensity_in.1, ...), custom_call_target="tpu_custom_call" | custom-call | tf_op jit(solution)/shard_map/tile_step/pallas_call | solution.py:371
  20.9 0.0 copy-done
  20.9 0.0 copy-done.1
  20.9 0.0 copy-done.2
  20.9 0.0 copy-done.3
  20.9 95.0 %field_step.1 = f32[2,512,512]{2,1,0:T(8,128)S(1)} custom-call(bf16[576,1280]{1,0:T(8,128)(2,1)S(1)} %get-tuple-element.9.z_hi, bf16[576,1280]{1,0:T(8,128)(2,1)S(1)} %get-tuple-element.10.z_lo, bf16[1280,1152]{1,0:T(8,128)(2,1)S(1)} %get-tuple-element.11.r_hi, bf16[1280,1152]{1,0:T(8,128)(2,1)S(1)} %get-tuple-element.12.r_lo, f32[4,32,128]{2,1,0:T(8,128)S(1)} %copy-done.3, ...), custom_call_target="tpu_custom_call" | custom-call | tf_op jit(solution)/shard_map/field_step/pallas_call | solution.py:768
  115.9 1.3 %copy.15 = f32[2,512,512]{2,1,0:T(8,128)} copy(f32[2,512,512]{2,1,0:T(8,128)S(1)} %field_step.1) | data formatting | bytes 4194304
Async XLA Ops:
  0.0 20.9 %copy-start = (bf16[4,256,256]{2,1,0:T(8,128)(2,1)S(1)}, bf16[4,256,256]{2,1,0:T(8,128)(2,1)}, u32[]{:S(2)}) copy-start(bf16[4,256,256]{2,1,0:T(8,128)(2,1)} %constant.26.clone.c_mats) | copy-start | bytes 1572868
  0.0 20.9 %copy-start.1 = (bf16[4,256,256]{2,1,0:T(8,128)(2,1)S(1)}, bf16[4,256,256]{2,1,0:T(8,128)(2,1)}, u32[]{:S(2)}) copy-start(bf16[4,256,256]{2,1,0:T(8,128)(2,1)} %constant.24.clone.r_mats) | copy-start | bytes 1572868
  0.0 20.9 %copy-start.2 = (f32[4,128,128]{2,1,0:T(8,128)S(1)}, f32[4,128,128]{2,1,0:T(8,128)}, u32[]{:S(2)}) copy-start(f32[4,128,128]{2,1,0:T(8,128)} %constant.25.clone.c_rows) | copy-start | bytes 786436
  0.0 20.9 %copy-start.3 = (f32[4,32,128]{2,1,0:T(8,128)S(1)}, f32[4,32,128]{2,1,0:T(8,128)}, u32[]{:S(2)}) copy-start(f32[4,32,128]{2,1,0:T(8,128)} %constant.23.clone.r_rows) | copy-start | bytes 196612

commit v7 on v6

--- a/solution.py
+++ b/solution.py
@@ -568,16 +568,15 @@
                 mid[4 * k + a, 0, at, :] = re
                 mid[4 * k + a, 1, at, :] = im
 
-        @pl.loop(0, 8)
-        def _(k):
+        for k in range(8):
             items = [(mid[4 * k + a, 0, at, :], mid[4 * k + a, 1, at, :]) for a in range(4)]
             done = fft_list(items, -1)
             for q in range(4):
                 index = k + 8 * q
-                tr = r_rows[0, pl.ds(index, 1), :]
-                ti = r_rows[1, pl.ds(index, 1), :]
+                tr = r_rows[0, index : index + 1, :]
+                ti = r_rows[1, index : index + 1, :]
                 re, im = cmul(*done[q], tr, ti)
-                start = pl.ds(pl.multiple_of(index * QUARTER, 8), 8)
+                start = slice(index * QUARTER, index * QUARTER + 8)
                 work[start, :128] = re
                 work[start, 128:] = im
 
@@ -590,14 +589,13 @@
 
         at = pl.ds(pl.multiple_of(quarter * QUARTER, 8), 8)
 
-        @pl.loop(0, 8)
-        def _(k):
+        for k in range(8):
             items = []
             for q in range(4):
                 index = k + 8 * q
-                tr = r_rows[0, pl.ds(index, 1), :]
-                ti = r_rows[1, pl.ds(index, 1), :]
-                start = pl.ds(pl.multiple_of(index * QUARTER, 8), 8)
+                tr = r_rows[0, index : index + 1, :]
+                ti = r_rows[1, index : index + 1, :]
+                start = slice(index * QUARTER, index * QUARTER + 8)
                 items.append(cmul(work[start, :128], work[start, 128:], tr, -ti))
             done = fft_list(items, 1)
             for a in range(4):

time: 117 us -> 117 us (level)
  no operation moved by 1% of the time
where the time goes in v7:
time: 117 us; the launch traced here: 116 us
  Pallas kernels  115 us (98%)
  local copies, waits for them, and re-layouts  1.34 us (1%)
    pallas_call x1, Pallas kernels, field_step(): pl.pallas_call(field_body, out_shape=jax.ShapeDtypeStruct((2, STRIDE, STR...  94.1 us
    pallas_call x1, Pallas kernels, tile_step(): pl.pallas_call(tile_body, out_shape=[jax.ShapeDtypeStruct((TILE, 2 * PAD)...  20.8 us

profile of v7, /device:TPU:1, one launch (start us, length us, event | category | flops | bytes accessed | tf_op | source)
XLA Modules:
  0.0 116.3 jit_solution(17281843262717343284)
XLA Ops:
  0.0 0.0 copy-start
  0.0 0.0 copy-start.1
  0.0 0.0 copy-start.2
  0.0 0.0 copy-start.3
  0.0 20.8 %tile_step.1 = (bf16[576,1280]{1,0:T(8,128)(2,1)S(1)}, bf16[576,1280]{1,0:T(8,128)(2,1)S(1)}, bf16[1280,1152]{1,0:T(8,128)(2,1)S(1)}, bf16[1280,1152]{1,0:T(8,128)(2,1)S(1)}) custom-call(s32[2,16]{1,0:T(2,128)} %bitcast.1, f32[2,576,576]{2,1,0:T(8,128)} %tiles_in.1, f32[2,128,128]{2,1,0:T(8,128)} %pupils_in.1, f32[16,128,128]{2,1,0:T(8,128)} %intensity_in.1, ...), custom_call_target="tpu_custom_call" | custom-call | tf_op jit(solution)/shard_map/tile_step/pallas_call | solution.py:371
  20.9 0.0 copy-done
  20.9 0.0 copy-done.1
  20.9 0.0 copy-done.2
  20.9 0.0 copy-done.3
  20.9 94.1 %field_step.1 = f32[2,512,512]{2,1,0:T(8,128)S(1)} custom-call(bf16[576,1280]{1,0:T(8,128)(2,1)S(1)} %get-tuple-element.9.z_hi, bf16[576,1280]{1,0:T(8,128)(2,1)S(1)} %get-tuple-element.10.z_lo, bf16[1280,1152]{1,0:T(8,128)(2,1)S(1)} %get-tuple-element.11.r_hi, bf16[1280,1152]{1,0:T(8,128)(2,1)S(1)} %get-tuple-element.12.r_lo, f32[4,32,128]{2,1,0:T(8,128)S(1)} %copy-done.3, ...), custom_call_target="tpu_custom_call" | custom-call | tf_op jit(solution)/shard_map/field_step/pallas_call | solution.py:766
  115.0 1.3 %copy.15 = f32[2,512,512]{2,1,0:T(8,128)} copy(f32[2,512,512]{2,1,0:T(8,128)S(1)} %field_step.1) | data formatting | bytes 4194304
Async XLA Ops:
  0.0 20.9 %copy-start = (bf16[4,256,256]{2,1,0:T(8,128)(2,1)S(1)}, bf16[4,256,256]{2,1,0:T(8,128)(2,1)}, u32[]{:S(2)}) copy-start(bf16[4,256,256]{2,1,0:T(8,128)(2,1)} %constant.26.clone.c_mats) | copy-start | bytes 1572868
  0.0 20.9 %copy-start.1 = (bf16[4,256,256]{2,1,0:T(8,128)(2,1)S(1)}, bf16[4,256,256]{2,1,0:T(8,128)(2,1)}, u32[]{:S(2)}) copy-start(bf16[4,256,256]{2,1,0:T(8,128)(2,1)} %constant.24.clone.r_mats) | copy-start | bytes 1572868
  0.0 20.9 %copy-start.2 = (f32[4,128,128]{2,1,0:T(8,128)S(1)}, f32[4,128,128]{2,1,0:T(8,128)}, u32[]{:S(2)}) copy-start(f32[4,128,128]{2,1,0:T(8,128)} %constant.25.clone.c_rows) | copy-start | bytes 786436
  0.0 20.9 %copy-start.3 = (f32[4,32,128]{2,1,0:T(8,128)S(1)}, f32[4,32,128]{2,1,0:T(8,128)}, u32[]{:S(2)}) copy-start(f32[4,32,128]{2,1,0:T(8,128)} %constant.23.clone.r_rows) | copy-start | bytes 196612
